TPU v7x, 128 devices: a whole 4x4x4 slice. The times are simulated.
128 devices in a mesh: ctx: 16 (over z, y), exp: 8 (over x, core).
Axes of the slice: x: 4, y: 4, z: 4, core: 2. Of those that a mesh axis runs over, the one named last changes fastest.
Arguments:
- query_states: bfloat16 [8, 2048, 4096], P('exp', 'ctx'), may hold values from -95 to 95
- key_states: bfloat16 [8, 2048, 256], P('exp', 'ctx'), may hold values from -4.5 to 4.5
- value_states: bfloat16 [8, 2048, 256], P('exp', 'ctx'), may hold values from -57 to 57
- positions: int32 [8, 2048], P('exp'), may hold values from 0 to 2047, as said below
- lengths: int32 [8, 16], P('exp'), may hold values from 1 to 512, 2048 in all within a row
- routes: int32 [8, 2048, 8], P('exp', 'ctx'), may hold values from 0 to 127, as said below
- gate_weights: float32 [8, 2048, 8], P('exp', 'ctx'), may hold values from 0.05 to 0.3
- norm_gain: float32 [4096], replicated, may hold values from 0.1 to 1.9
- gate_proj: bfloat16 [128, 4096, 768], P(('ctx', 'exp')), may hold values from -0.09375 to 0.09375
- up_proj: bfloat16 [128, 4096, 768], P(('ctx', 'exp')), may hold values from -0.09375 to 0.09375
- down_proj: bfloat16 [128, 768, 4096], P(('ctx', 'exp')), may hold values from -0.21875 to 0.21875
Outputs:
- layer_out: bfloat16 [8, 2048, 4096], P('exp', 'ctx')
Inputs may be any that keep to these rules, and one draw needn't show every extreme that they name: In each pack every position 0 to 2047 stands in one slot; the 128 slots of one device hold two runs of 64 consecutive positions. `routes`: each row names 8 different experts; at most 10 rows of one device name the same expert, and one expert is named by exactly 10 rows of every device.
All inputs are finite; a program needn't handle non-finite values.
Results may differ from a plain program's by a relative error of at most 0.011.
Values may be sent and summed in bfloat16 or wider, within the bound.
A program may use at most 128 MiB of HBM per device.

v0:
```python
import math

import jax
import jax.numpy as jnp
from jax import lax
from jax.sharding import PartitionSpec as P

QH = 32
KVH = 2
HD = 128
TOP = 8


neg_large = -1e30
norm_eps = 1e-06


def doc_index(places, lengths):
    doc_ends = jnp.cumsum(lengths)
    return jnp.sum((doc_ends[None, :] <= places[:, None]).astype(jnp.int32), axis=1)


def expert_apply(token_rows, gate_matrix, up_matrix, down_matrix):
    gate_act = jnp.dot(token_rows, gate_matrix, preferred_element_type=jnp.float32)
    up_act = jnp.dot(token_rows, up_matrix, preferred_element_type=jnp.float32)
    hidden = (jax.nn.silu(gate_act) * up_act).astype(jnp.bfloat16)
    return jnp.dot(hidden, down_matrix, preferred_element_type=jnp.float32).astype(jnp.bfloat16)


def online_block(carried, queries, key_block, value_block, visible):
    maxima, totals, summed = carried
    scores = jnp.einsum(
        "igqd,jgd->gqij", queries, key_block, preferred_element_type=jnp.float32
    ) * (1.0 / math.sqrt(HD))
    scores = jnp.where(visible[None, None], scores, neg_large)
    fresh_max = jnp.maximum(maxima, jnp.max(scores, axis=3))
    factor = jnp.exp(maxima - fresh_max)
    exp_terms = jnp.where(visible[None, None], jnp.exp(scores - fresh_max[..., None]), 0.0)
    totals = totals * factor + jnp.sum(exp_terms, axis=3)
    summed = summed * factor[..., None] + jnp.einsum(
        "gqij,jgd->gqid",
        exp_terms.astype(jnp.bfloat16),
        value_block,
        preferred_element_type=jnp.float32,
    )
    return (fresh_max, totals, summed)


def attention_keys(query_states, key_states, value_states, pack_places, pack_docs):
    tokens = query_states.shape[1]
    per_group = QH // KVH
    queries = query_states[0].reshape(tokens, KVH, per_group, HD)
    start_own = lax.axis_index("ctx") * tokens
    own_places = lax.dynamic_slice_in_dim(pack_places, start_own, tokens)
    own_docs = lax.dynamic_slice_in_dim(pack_docs, start_own, tokens)
    initial = (
        jnp.full((KVH, per_group, tokens), neg_large, jnp.float32),
        jnp.zeros((KVH, per_group, tokens), jnp.float32),
        jnp.zeros((KVH, per_group, tokens, HD), jnp.float32),
    )
    carried = initial
    key_piece = lax.all_gather(key_states, "ctx", axis=1, tiled=True)
    value_piece = lax.all_gather(value_states, "ctx", axis=1, tiled=True)
    row_count = key_piece.shape[1]
    stride = math.gcd(row_count, 512)
    block_count = row_count // stride
    key_blocks = key_piece.reshape(block_count, stride, KVH, HD)
    value_blocks = value_piece.reshape(block_count, stride, KVH, HD)
    place_blocks = pack_places.reshape(block_count, stride)
    doc_blocks = pack_docs.reshape(block_count, stride)

    def scan_block(inner_carry, blocks):
        key_block, value_block, places, doc_ids = blocks
        visible = (doc_ids[None, :] == own_docs[:, None]) & (places[None, :] <= own_places[:, None])
        return (online_block(inner_carry, queries, key_block, value_block, visible), None)

    carried, ignored = lax.scan(
        scan_block, carried, (key_blocks, value_blocks, place_blocks, doc_blocks)
    )
    maxima, totals, summed = carried
    attended = summed / totals[..., None]
    return jnp.transpose(attended, (2, 0, 1, 3)).reshape(tokens, QH * HD).astype(jnp.bfloat16)


def local(
    query_states,
    key_states,
    value_states,
    positions,
    lengths,
    routes,
    gate_weights,
    norm_gain,
    gate_proj,
    up_proj,
    down_proj,
):
    pack_places = positions[0]
    pack_docs = doc_index(pack_places, lengths[0])
    attended = attention_keys(query_states, key_states, value_states, pack_places, pack_docs)
    widened = attended.astype(jnp.float32)
    normed = (
        widened
        * lax.rsqrt(jnp.mean(widened * widened, axis=1, keepdims=True) + norm_eps)
        * norm_gain
    ).astype(jnp.bfloat16)
    tokens = attended.shape[0]
    feature_count = attended.shape[1]
    experts_count = lax.axis_size(("ctx", "exp"))
    mean_load = tokens * TOP // experts_count
    capacity = mean_load + max(2, mean_load // 4)
    flat_experts = routes[0].reshape(tokens * TOP)
    one_hot = (flat_experts[:, None] == jnp.arange(experts_count)[None, :]).astype(jnp.int32)
    slot_ranks = jnp.sum((jnp.cumsum(one_hot, axis=0) - one_hot) * one_hot, axis=1)
    slot_ids = flat_experts * capacity + slot_ranks
    source_rows = jnp.arange(tokens * TOP) // TOP
    row_table = jnp.zeros((experts_count * capacity,), jnp.int32).at[slot_ids].set(source_rows)
    filled = jnp.zeros((experts_count * capacity,), jnp.bool_).at[slot_ids].set(True)
    outgoing = jnp.where(filled[:, None], normed[row_table], jnp.zeros((), jnp.bfloat16)).reshape(
        experts_count, capacity, feature_count
    )
    gate_matrix = gate_proj[0]
    up_matrix = up_proj[0]
    down_matrix = down_proj[0]
    arrived = lax.all_to_all(outgoing, ("ctx", "exp"), split_axis=0, concat_axis=0, tiled=True)
    sources, slots_here, width_here = arrived.shape
    results = expert_apply(
        arrived.reshape(sources * slots_here, width_here), gate_matrix, up_matrix, down_matrix
    )
    returned = lax.all_to_all(
        results.reshape(sources, slots_here, width_here),
        ("ctx", "exp"),
        split_axis=0,
        concat_axis=0,
        tiled=True,
    )
    returned = returned.reshape(experts_count * capacity, feature_count)
    pulled = returned[slot_ids].reshape(tokens, TOP, feature_count)
    mixed_out = widened + jnp.einsum(
        "tk,tkd->td", gate_weights[0], pulled, preferred_element_type=jnp.float32
    )
    return mixed_out.astype(jnp.bfloat16).reshape(1, tokens, feature_count)


def solution(mesh):
    in_specs = (
        P("exp", "ctx", None),
        P("exp", "ctx", None),
        P("exp", "ctx", None),
        P("exp", None),
        P("exp", None),
        P("exp", "ctx", None),
        P("exp", "ctx", None),
        P(),
        P(("ctx", "exp"), None, None),
        P(("ctx", "exp"), None, None),
        P(("ctx", "exp"), None, None),
    )
    out_specs = P("exp", "ctx", None)
    return jax.shard_map(local, mesh=mesh, in_specs=in_specs, out_specs=out_specs, check_vma=False)
```

profile of v0, /device:TPU:32, one launch (start us, length us, event | category | flops | bytes accessed | tf_op | source)
XLA Modules:
  0.0 763.1 jit_solution(12737842680979054659)
XLA Ops:
  6.5 0.7 all-gather.3.cloned.1.call-update
  7.3 0.7 all-gather.5.cloned.1.call-update
  8.0 0.8 copy.35
  9.0 0.7 copy.28
  9.9 0.8 convert_reduce_fusion
  10.7 0.7 dynamic_slice.26
  11.4 1.6 copy.29
  13.0 0.7 copy.31
  13.7 0.5 broadcast.172
  14.2 1.4 reduce.6
  16.3 0.4 fusion.33
  16.7 4.3 scatter_custom_fusion.1
  21.0 4.5 scatter_custom_fusion
  25.7 1.1 dynamic-slice_bitcast_fusion
  26.9 0.6 pad_clamp_fusion
  27.5 26.6 %all-gather.3.cloned.1.call-done = bf16[1,2048,256]{2,1,0:T(8,128)(2,1)} async-done(((bf16[1,128,256]{2,1,0:T(8,128)(2,1)}), bf16[1,2048,256]{2,1,0:T(8,128)(2,1)}) %all-gather.3.cloned.1.call-update) | async-done | bytes 1048592 | tf_op jit(solution)/shard_map/all_gather | solution.py:62
  54.1 1.3 reshape.179
  55.4 42.9 %all-gather.5.cloned.1.call-done = bf16[1,2048,256]{2,1,0:T(8,128)(2,1)} async-done(((bf16[1,128,256]{2,1,0:T(8,128)(2,1)}), bf16[1,2048,256]{2,1,0:T(8,128)(2,1)}) %all-gather.5.cloned.1.call-update) | async-done | bytes 1048592 | tf_op jit(solution)/shard_map/all_gather | solution.py:63
  98.4 1.3 reshape.180
  99.7 67.1 %while.15 = (s32[]{:T(128)}, f32[2,16,128]{2,1,0:T(8,128)S(1)}, f32[2,16,128]{2,1,0:T(8,128)S(1)}, f32[2,16,128,128]{3,2,1,0:T(8,128)}, s32[4,512]{1,0:T(4,128)S...) while((s32[]{:T(128)}, f32[2,16,128]{2,1,0:T(8,128)S(1)}, ...), condition=%wide.region_5.6_spmd.clone, body=%wide.region_2.5_spmd.clone.sunk | while | flops 1102794752 | bytes 66073772 | solution.py:77
  99.7 0.9 compare_and_fusion.2
  100.6 0.4 constant_dynamic-slice_fusion.7
  101.0 4.6 fusion.57
  105.6 4.7 fusion.58
  110.2 1.1 copy-done
  111.4 4.2 fusion.60
  115.6 0.9 compare_and_fusion.2
  116.5 0.4 constant_dynamic-slice_fusion.7
  116.9 4.5 fusion.57
  121.4 4.7 fusion.58
  126.1 1.1 copy-done
  127.2 5.4 fusion.60
  132.7 0.9 compare_and_fusion.2
  133.6 0.4 constant_dynamic-slice_fusion.7
  133.9 4.5 fusion.57
  138.5 4.7 fusion.58
  143.2 1.1 copy-done
  144.3 5.4 fusion.60
  149.8 0.9 compare_and_fusion.2
  150.6 0.4 constant_dynamic-slice_fusion.7
  151.0 4.6 fusion.57
  155.6 4.7 fusion.58
  160.3 1.1 copy-done
  161.4 5.4 fusion.60
  166.8 2.1 fusion.27
  168.9 0.2 convert_bitcast_fusion
  169.2 1.2 copy.33
  170.4 1.3 copy-done.1
  171.7 1.8 fusion.29
  173.6 8.4 %gather_fusion = bf16[1280,4096]{1,0:T(8,128)(2,1)} fusion(bf16[128,4096]{1,0:T(8,128)(2,1)S(1)} %fusion.29, s32[2048]{0:T(1024)S(1)} %copy-done.4), kind=kCustom, calls=%fused_computation | custom fusion | bytes 20976640 | tf_op jit(solution)/shard_map/gather | solution.py:119
  181.9 15.2 %gather.9 = bf16[128,10,4096]{2,1,0:T(8,128)(2,1)} reshape(bf16[1280,4096]{1,0:T(8,128)(2,1)} %gather_fusion) | data formatting | bytes 20971520 | tf_op jit(solution)/shard_map/gather | solution.py:119
  197.1 8.3 %broadcast_select_fusion = bf16[128,10,4096]{2,1,0:T(8,128)(2,1)S(1)} fusion(bf16[128,10,4096]{2,1,0:T(8,128)(2,1)} %gather.9, pred[128,10]{1,0:T(8,128)(4,1)S(1)} %broadcast_in_dim.72), kind=kLoop, calls=%fused_computation.28 | loop fusion | flops 5242880 | bytes 20972800 | tf_op jit(solution)/shard_map/jit(_where)/select_n | solution.py:119
  205.4 194.8 %all_to_all.10 = bf16[128,10,4096]{2,1,0:T(8,128)(2,1)} all-to-all(bf16[128,10,4096]{2,1,0:T(8,128)(2,1)S(1)} %broadcast_select_fusion), channel_id=1, replica_groups=mesh['ctx'=16,'exp'=8] {'ctx','exp'}, dimensions={0} | all-to-all | bytes 20971520 | tf_op jit(solution)/shard_map/all_to_all | solution.py:125
  400.2 16.7 %reshape.182 = bf16[1280,4096]{1,0:T(8,128)(2,1)} reshape(bf16[128,10,4096]{2,1,0:T(8,128)(2,1)} %all_to_all.10) | data formatting | bytes 20971520 | tf_op jit(solution)/shard_map/reshape | solution.py:128
  416.9 12.3 %fusion.19 = f32[1280,768]{1,0:T(8,128)S(1)} fusion(bf16[1280,4096]{1,0:T(8,128)(2,1)} %reshape.182, bf16[1,4096,768]{2,1,0:T(8,128)(2,1)} %param.21), kind=kOutput, calls=%fused_computation.35 | convolution fusion | flops 8053063680 | bytes 20709376 | tf_op jit(solution)/shard_map/dot_general | solution.py:24
  429.2 9.0 %fusion.24 = bf16[1280,768]{1,0:T(8,128)(2,1)S(1)} fusion(bf16[1280,4096]{1,0:T(8,128)(2,1)S(1)} %copy-done.3, bf16[1,4096,768]{2,1,0:T(8,128)(2,1)S(1)} %bitcast.119, f32[1280,768]{1,0:T(8,128)S(1)} %fusion.19), kind=kOutput, calls=%fused_computation.38 | convolution fusion | flops 8058961920 | bytes 22675456 | tf_op jit(solution)/shard_map/dot_general | solution.py:25
  438.2 13.8 %convolution_convert_fusion = bf16[1280,4096]{1,0:T(8,128)(2,1)} fusion(bf16[1280,768]{1,0:T(8,128)(2,1)S(1)} %fusion.24, bf16[1,768,4096]{2,1,0:T(8,128)(2,1)} %param.23), kind=kOutput, calls=%fused_computation.29 | convolution fusion | flops 8058306560 | bytes 18743296 | tf_op jit(solution)/shard_map/dot_general | solution.py:27
  452.0 15.2 %reshape.183 = bf16[128,10,4096]{2,1,0:T(8,128)(2,1)} reshape(bf16[1280,4096]{1,0:T(8,128)(2,1)} %convolution_convert_fusion) | data formatting | bytes 20971520 | tf_op jit(solution)/shard_map/reshape | solution.py:131
  467.2 6.9 all-to-all-start.1
  474.2 232.6 %all-to-all-done.1 = bf16[128,10,4096]{2,1,0:T(8,128)(2,1)} async-done(((bf16[128,10,4096]{2,1,0:T(8,128)(2,1)}), bf16[128,10,4096]{2,1,0:T(8,128)(2,1)}, u32[]{:S(2)}, u32[]{:S(2)}) %all-to-all-start.1) | async-done | bytes 10485792 | tf_op jit(solution)/shard_map/all_to_all | solution.py:130
  706.9 16.5 %reshape.184 = bf16[1280,4096]{1,0:T(8,128)(2,1)} reshape(bf16[128,10,4096]{2,1,0:T(8,128)(2,1)} %all-to-all-done.1) | data formatting | bytes 20971520 | tf_op jit(solution)/shard_map/reshape | solution.py:137
  723.4 20.4 %gather_fusion.1 = bf16[1024,4096]{1,0:T(8,128)(2,1)} fusion(bf16[1280,4096]{1,0:T(8,128)(2,1)} %reshape.184, s32[1024]{0:T(1024)S(1)} %broadcast_clamp_fusion), kind=kCustom, calls=%fused_computation.1 | custom fusion | bytes 16781312 | tf_op jit(solution)/shard_map/gather | solution.py:138
  743.8 7.2 fusion.14
  751.0 4.8 fusion.31
  (71 shorter events, 1.6 us)
Async XLA Ops:
  6.5 9.5 %copy-start.6 = (s32[1,128,8]{1,2,0:T(8,128)S(1)}, s32[1,128,8]{1,2,0:T(8,128)}, u32[]{:S(2)}) copy-start(s32[1,128,8]{1,2,0:T(8,128)} %param.18) | copy-start | bytes 12292
  6.5 47.5 %all-gather.3.cloned.1.call-start = ((), (), s32[]{:S(2)}) async-start(), calls=%async_computation.2 | async-start | bytes 1114112 | tf_op jit(solution)/shard_map/all_gather | solution.py:62
  7.3 91.1 %all-gather.5.cloned.1.call-start = ((), (), s32[]{:S(2)}) async-start(), calls=%async_computation.3 | async-start | bytes 1114112 | tf_op jit(solution)/shard_map/all_gather | solution.py:63
  16.7 4.3 copy-start.7
  105.5 5.8 copy-start
  121.4 5.8 copy-start
  138.5 5.8 copy-start
  155.6 5.8 copy-start
  166.8 4.9 copy-start.5
  166.8 6.8 copy-start.4
  170.4 1.3 copy-start.1
  400.2 29.0 %slice-start = ((s8[6291456]{0:T(1024)(128)(4,1)}), s8[2097152]{0:T(1024)(128)(4,1)S(1)}, s32[]{:S(2)}) async-start(s8[6291456]{0:T(1024)(128)(4,1)} %bitcast.118), calls=%async_computation.4 | async-start | bytes 4194304
  416.9 12.3 %copy-start.3 = (bf16[1280,4096]{1,0:T(8,128)(2,1)S(1)}, bf16[1280,4096]{1,0:T(8,128)(2,1)}, u32[]{:S(2)}) copy-start(bf16[1280,4096]{1,0:T(8,128)(2,1)} %reshape.182) | copy-start | bytes 31457284
  416.9 12.3 %slice-start.1 = ((s8[6291456]{0:T(1024)(128)(4,1)}), s8[4194304]{0:T(1024)(128)(4,1)S(1)}, s32[]{:S(2)}) async-start(s8[6291456]{0:T(1024)(128)(4,1)} %bitcast.118), calls=%async_computation.5 | async-start | bytes 8388608
  467.2 6.9 copy-start.9
  467.2 7.1 copy-start.8
  467.2 239.7 %all-to-all-start.1 = ((bf16[128,10,4096]{2,1,0:T(8,128)(2,1)}), bf16[128,10,4096]{2,1,0:T(8,128)(2,1)}, u32[]{:S(2)}, u32[]{:S(2)}) async-start(bf16[128,10,4096]{2,1,0:T(8,128)(2,1)} %reshape.183), calls=%async_computation.1 | async-start | bytes 33554432 | tf_op jit(solution)/shard_map/all_to_all | solution.py:130
  743.8 7.2 copy-start.2
Sparse Core Ops, SparseCore 0:
  9.5 44.5 all-gather.2
  56.2 42.0 all-gather.4
where the time goes:
time: 778 us; the launch traced here: 763 us
  waiting for transfers between devices  304 us (39%)
  blocking collectives  195 us (25%)
  local copies, waits for them, and re-layouts  120 us (15%)
  matrix products  80.9 us (10%)
  other arithmetic  43 us (6%)
  between operations  14.2 us (2%)
    all_to_all x1, waiting for transfers between devices, local(): lax.all_to_all(results.reshape(sources, slots_here, width_here), ('ctx',...  233 us
    all_to_all x1, blocking collectives, local(): lax.all_to_all(outgoing, ('ctx', 'exp'), split_axis=0, concat_axis=0, til...  195 us
    all_gather x1, waiting for transfers between devices, attention_keys(): value_piece = lax.all_gather(value_states, 'ctx', axis=1, tiled=True)  42.9 us
    all_gather x1, waiting for transfers between devices, attention_keys(): key_piece = lax.all_gather(key_states, 'ctx', axis=1, tiled=True)  26.6 us
    gather x2, local copies, waits for them, and re-layouts, local(): normed[row_table]  23.6 us
    dot_general x4, matrix products, online_block(): jnp.einsum('gqij,jgd->gqid', exp_terms.astype(jnp.bfloat16), value_block,...  20.5 us
    gather x1, local copies, waits for them, and re-layouts, local(): pulled = returned[slot_ids].reshape(tokens, TOP, feature_count)  20.4 us
    reduce_sum x4, other arithmetic, online_block(): totals = totals * factor + jnp.sum(exp_terms, axis=3)  18.6 us
  transfers between devices with their start and end apart: 3, of which 3 were waited for; matrix products, arithmetic and copies ran while one was open for 3% of the time, Pallas kernels for 0%

commit v1 on v0

v1 whole, which is shorter than its diff:
```python
import functools
import math

import jax
import jax.numpy as jnp
from jax import lax
from jax.experimental import pallas as pl
from jax.experimental.pallas import tpu as pltpu
from jax.sharding import PartitionSpec as P

QH = 32
HD = 128
D = 4096
HID = 768
TOK = 128
N_CTX = 16
N_EXP = 8
N_DEV = 128
SEQ = 2048
DOCS = 16
RUN = 64
BLOCKS = SEQ // RUN
WINDOW = 10
KEYS = WINDOW * RUN
QUARTER = D // 4
GROUP = 32
STRIDE = 37
MESH = pl.DeviceIdType.MESH

neg_large = -1e30
norm_eps = 1e-06


def peer(ctx, exp, delta):
    z, y, x, core = ctx // 4, ctx % 4, exp // 2, exp % 2
    dz, dy, dx, dcore = delta // 32, (delta // 8) % 4, (delta // 2) % 4, delta % 2
    return (
        ((z + dz) % 4) * 4 + (y + dy) % 4,
        ((x + dx) % 4) * 2 + (core + dcore) % 2,
    )


def gather_kernel(k_ref, v_ref, out_ref, send_sem, recv_sem, local_sem):
    ctx = lax.axis_index("ctx")
    exp = lax.axis_index("exp")
    barrier = pltpu.get_barrier_semaphore()
    peers = [lax.rem(ctx + step, N_CTX) for step in range(1, N_CTX)]
    for target in peers:
        pl.semaphore_signal(barrier, inc=1, device_id=(target, exp), device_id_type=MESH)
    pl.semaphore_wait(barrier, N_CTX - 1)
    copies = []
    for step, target in enumerate(peers):
        for which, source in enumerate((k_ref, v_ref)):
            copies.append(
                pltpu.make_async_remote_copy(
                    src_ref=source,
                    dst_ref=out_ref.at[ctx, which],
                    send_sem=send_sem.at[step, which],
                    recv_sem=recv_sem.at[step, which],
                    device_id=(target, exp),
                    device_id_type=MESH,
                )
            )
    for copy in copies:
        copy.start()
    own = [
        pltpu.make_async_copy(source, out_ref.at[ctx, which], local_sem.at[which])
        for which, source in enumerate((k_ref, v_ref))
    ]
    for copy in own:
        copy.start()
    for copy in copies:
        copy.wait()
    for copy in own:
        copy.wait()


def gather_keys(keys, values):
    return pl.pallas_call(
        gather_kernel,
        out_shape=jax.ShapeDtypeStruct((N_CTX, 2, TOK, 256), jnp.bfloat16),
        in_specs=[pl.BlockSpec(memory_space=pltpu.VMEM)] * 2,
        out_specs=pl.BlockSpec(memory_space=pltpu.VMEM),
        scratch_shapes=[
            pltpu.SemaphoreType.DMA((N_CTX - 1, 2)),
            pltpu.SemaphoreType.DMA((N_CTX - 1, 2)),
            pltpu.SemaphoreType.DMA((2,)),
        ],
        compiler_params=pltpu.CompilerParams(collective_id=0, has_side_effects=True),
        name="gather_keys",
    )(keys, values)


def attend_kernel(
    pos_ref, len_ref, q_ref, kv_ref, gain_ref, att_ref, norm_ref, where_ref, k_win, v_win
):
    ctx = lax.axis_index("ctx")
    for block in range(BLOCKS):
        where_ref[pos_ref[0, RUN * block] // RUN] = block
    ends = []
    total = jnp.int32(0)
    for doc in range(DOCS):
        total = total + len_ref[0, doc]
        ends.append(total)

    def one_run(run, carry):
        first_block = pos_ref[0, ctx * TOK + run * RUN] // RUN
        for step in range(WINDOW):
            block = where_ref[jnp.maximum(first_block - (WINDOW - 1) + step, 0)]
            rows = pl.ds(pl.multiple_of((block % 2) * RUN, RUN), RUN)
            k_win[pl.ds(step * RUN, RUN), :] = kv_ref[block // 2, 0, rows, :]
            v_win[pl.ds(step * RUN, RUN), :] = kv_ref[block // 2, 1, rows, :]
        own = first_block * RUN + lax.broadcasted_iota(jnp.int32, (RUN, 1), 0)
        start = jnp.zeros((RUN, 1), jnp.int32)
        for end in ends:
            start = jnp.maximum(start, jnp.where(own >= end, end, 0))
        places = (first_block - (WINDOW - 1)) * RUN + lax.broadcasted_iota(
            jnp.int32, (RUN, KEYS), 1
        )
        visible = (places >= start) & (places <= own)
        tokens = pl.ds(pl.multiple_of(run * RUN, RUN), RUN)

        def four_heads(part, inner):
            group = part // 4
            lanes = pl.ds(pl.multiple_of(group * HD, HD), HD)
            queries = jnp.concatenate(
                [
                    q_ref[tokens, pl.ds(pl.multiple_of((part * 4 + i) * HD, HD), HD)]
                    for i in range(4)
                ],
                axis=0,
            )
            scores = lax.dot_general(
                queries,
                k_win[:, lanes],
                (((1,), (1,)), ((), ())),
                preferred_element_type=jnp.float32,
            )
            scores = jnp.where(visible[None], scores.reshape(4, RUN, KEYS), neg_large)
            maxima = jnp.max(scores, axis=2, keepdims=True)
            probs = jnp.exp((scores - maxima) * (1.0 / math.sqrt(HD)))
            totals = jnp.sum(probs, axis=2, keepdims=True)
            summed = jnp.dot(
                probs.reshape(4 * RUN, KEYS).astype(jnp.bfloat16),
                v_win[:, lanes],
                preferred_element_type=jnp.float32,
            )
            result = (summed.reshape(4, RUN, HD) / totals).astype(jnp.bfloat16)
            for i in range(4):
                att_ref[tokens, pl.ds(pl.multiple_of((part * 4 + i) * HD, HD), HD)] = result[i]
            return inner

        lax.fori_loop(0, QH // 4, four_heads, 0)
        wide = att_ref[tokens, :].astype(jnp.float32)
        scale = lax.rsqrt(jnp.mean(wide * wide, axis=1, keepdims=True) + norm_eps)
        norm_ref[tokens, :] = (wide * scale * gain_ref[...]).astype(jnp.bfloat16)
        return carry

    lax.fori_loop(0, TOK // RUN, one_run, 0)


def attend(positions, lengths, queries, gathered, gain):
    return pl.pallas_call(
        attend_kernel,
        out_shape=[jax.ShapeDtypeStruct((TOK, D), jnp.bfloat16)] * 2,
        in_specs=[pl.BlockSpec(memory_space=pltpu.SMEM)] * 2
        + [pl.BlockSpec(memory_space=pltpu.VMEM)] * 3,
        out_specs=[pl.BlockSpec(memory_space=pltpu.VMEM)] * 2,
        scratch_shapes=[
            pltpu.SMEM((BLOCKS,), jnp.int32),
            pltpu.VMEM((KEYS, 256), jnp.bfloat16),
            pltpu.VMEM((KEYS, 256), jnp.bfloat16),
        ],
        name="attend",
    )(positions, lengths, queries, gathered, gain)


def slots_by_expert(routes_ref):
    experts = lax.broadcasted_iota(jnp.int32, (N_DEV, TOK), 0)
    named = jnp.zeros((N_DEV, TOK), jnp.float32)
    for k in range(8):
        named = named + (routes_ref[k : k + 1, :] == experts).astype(jnp.float32)
    earlier = (
        lax.broadcasted_iota(jnp.int32, (TOK, TOK), 0)
        < lax.broadcasted_iota(jnp.int32, (TOK, TOK), 1)
    ).astype(jnp.bfloat16)
    ranks = jnp.dot(named.astype(jnp.bfloat16), earlier, preferred_element_type=jnp.float32)
    return jnp.where(named > 0.5, ranks.astype(jnp.int32), -1)


def main_slots(slots):
    wide = jnp.broadcast_to(slots[:, None, :], (GROUP, 8, TOK))
    return (wide == lax.broadcasted_iota(jnp.int32, (GROUP, 8, TOK), 1)).reshape(GROUP * 8, TOK)


def extra_slots(slots, quarter):
    wide = jnp.broadcast_to(slots[:, None, :], (GROUP, 8, TOK))
    row = lax.broadcasted_iota(jnp.int32, (GROUP, 8, TOK), 1)
    hit = (wide == 8 + row % 2) & (row // 2 == quarter)
    return hit.reshape(GROUP * 8, TOK)


def pack_kernel(routes_ref, norm_ref, out_ref, slot_ref):
    step = pl.program_id(0)

    @pl.when(step == 0)
    def _():
        slot_ref[...] = slots_by_expert(routes_ref)

    slots = slot_ref[pl.ds(pl.multiple_of(step * GROUP, GROUP), GROUP), :]
    main = main_slots(slots).astype(jnp.float32).astype(jnp.bfloat16)
    extra = jnp.zeros((GROUP * 8, QUARTER), jnp.float32)
    for quarter in range(4):
        part = norm_ref[:, quarter * QUARTER : (quarter + 1) * QUARTER]
        rows = jnp.dot(main, part, preferred_element_type=jnp.float32)
        out_ref[:, quarter] = rows.astype(jnp.bfloat16).reshape(GROUP, 8, QUARTER)
        chosen = extra_slots(slots, quarter).astype(jnp.float32).astype(jnp.bfloat16)
        extra = extra + jnp.dot(chosen, part, preferred_element_type=jnp.float32)
    out_ref[:, 4] = extra.astype(jnp.bfloat16).reshape(GROUP, 8, QUARTER)


def pack(routes, normed):
    return pl.pallas_call(
        pack_kernel,
        grid=(N_DEV // GROUP,),
        out_shape=jax.ShapeDtypeStruct((N_DEV, 5, 8, QUARTER), jnp.bfloat16),
        in_specs=[
            pl.BlockSpec((8, TOK), lambda i: (0, 0)),
            pl.BlockSpec((TOK, D), lambda i: (0, 0)),
        ],
        out_specs=pl.BlockSpec((GROUP, 5, 8, QUARTER), lambda i: (i, 0, 0, 0)),
        scratch_shapes=[pltpu.VMEM((N_DEV, TOK), jnp.int32)],
        compiler_params=pltpu.CompilerParams(vmem_limit_bytes=40 << 20),
        name="pack_rows",
    )(routes, normed)


def exchange_kernel(in_ref, out_ref, send_sem, recv_sem, local_sem):
    ctx = lax.axis_index("ctx")
    exp = lax.axis_index("exp")
    me = ctx * N_EXP + exp
    barrier = pltpu.get_barrier_semaphore()

    def greet(delta, carry):
        pl.semaphore_signal(
            barrier, inc=1, device_id=peer(ctx, exp, delta), device_id_type=MESH
        )
        return carry

    lax.fori_loop(1, N_DEV, greet, 0)
    pl.semaphore_wait(barrier, N_DEV - 1)

    def message(i):
        delta = (i * STRIDE) % N_DEV
        target = peer(ctx, exp, delta)
        return pltpu.make_async_remote_copy(
            src_ref=in_ref.at[target[0] * N_EXP + target[1]],
            dst_ref=out_ref.at[me],
            send_sem=send_sem.at[delta],
            recv_sem=recv_sem.at[delta],
            device_id=target,
            device_id_type=MESH,
        )

    def send(i, carry):
        message(i).start()
        return carry

    def finish(i, carry):
        message(i).wait()
        return carry

    lax.fori_loop(1, N_DEV, send, 0)
    own = pltpu.make_async_copy(in_ref.at[me], out_ref.at[me], local_sem)
    own.start()
    lax.fori_loop(1, N_DEV, finish, 0)
    own.wait()


def exchange(messages, collective_id):
    return pl.pallas_call(
        exchange_kernel,
        out_shape=jax.ShapeDtypeStruct(messages.shape, messages.dtype),
        in_specs=[pl.BlockSpec(memory_space=pltpu.HBM)],
        out_specs=pl.BlockSpec(memory_space=pltpu.HBM),
        scratch_shapes=[
            pltpu.SemaphoreType.DMA((N_DEV,)),
            pltpu.SemaphoreType.DMA((N_DEV,)),
            pltpu.SemaphoreType.DMA,
        ],
        compiler_params=pltpu.CompilerParams(
            collective_id=collective_id, has_side_effects=True
        ),
        name="exchange_%d" % collective_id,
    )(messages)


def extra_pick(quarter):
    row = lax.broadcasted_iota(jnp.int32, (GROUP * 2, GROUP * 8), 0)
    column = lax.broadcasted_iota(jnp.int32, (GROUP * 2, GROUP * 8), 1)
    hit = column == (row // 2) * 8 + quarter * 2 + row % 2
    return hit.astype(jnp.float32).astype(jnp.bfloat16)


def expert_kernel(in_ref, gate_ref, up_ref, down_ref, out_ref):
    packed = in_ref[:, 4].reshape(GROUP * 8, QUARTER)
    gate = jnp.zeros((GROUP * 10, HID), jnp.float32)
    up = jnp.zeros((GROUP * 10, HID), jnp.float32)
    for quarter in range(4):
        extra = jnp.dot(extra_pick(quarter), packed, preferred_element_type=jnp.float32)
        rows = jnp.concatenate(
            [in_ref[:, quarter].reshape(GROUP * 8, QUARTER), extra.astype(jnp.bfloat16)], axis=0
        )
        span = slice(quarter * QUARTER, (quarter + 1) * QUARTER)
        gate = gate + jnp.dot(rows, gate_ref[span, :], preferred_element_type=jnp.float32)
        up = up + jnp.dot(rows, up_ref[span, :], preferred_element_type=jnp.float32)
    hidden = (gate / (1.0 + jnp.exp(-gate)) * up).astype(jnp.bfloat16)
    spread = jnp.zeros((GROUP * 8, QUARTER), jnp.float32)
    for quarter in range(4):
        span = slice(quarter * QUARTER, (quarter + 1) * QUARTER)
        result = jnp.dot(hidden, down_ref[:, span], preferred_element_type=jnp.float32)
        result = result.astype(jnp.bfloat16)
        out_ref[:, quarter] = result[: GROUP * 8].reshape(GROUP, 8, QUARTER)
        spread = spread + lax.dot_general(
            extra_pick(quarter),
            result[GROUP * 8 :],
            (((0,), (0,)), ((), ())),
            preferred_element_type=jnp.float32,
        )
    out_ref[:, 4] = spread.astype(jnp.bfloat16).reshape(GROUP, 8, QUARTER)


def expert(messages, gate, up, down):
    block = pl.BlockSpec((GROUP, 5, 8, QUARTER), lambda i: (i, 0, 0, 0))
    return pl.pallas_call(
        expert_kernel,
        grid=(N_DEV // GROUP,),
        out_shape=jax.ShapeDtypeStruct(messages.shape, messages.dtype),
        in_specs=[
            block,
            pl.BlockSpec((D, HID), lambda i: (0, 0), pipeline_mode=pl.Buffered(1)),
            pl.BlockSpec((D, HID), lambda i: (0, 0), pipeline_mode=pl.Buffered(1)),
            pl.BlockSpec((HID, D), lambda i: (0, 0), pipeline_mode=pl.Buffered(1)),
        ],
        out_specs=block,
        compiler_params=pltpu.CompilerParams(vmem_limit_bytes=56 << 20),
        name="expert",
    )(messages, gate, up, down)


def combine_kernel(routes_ref, gates_ref, att_ref, in_ref, out_ref, slot_ref, weight_ref, sum_ref):
    step = pl.program_id(0)

    @pl.when(step == 0)
    def _():
        slot_ref[...] = slots_by_expert(routes_ref)
        experts = lax.broadcasted_iota(jnp.int32, (N_DEV, TOK), 0)
        weight = jnp.zeros((N_DEV, TOK), jnp.float32)
        for k in range(8):
            weight = weight + jnp.where(
                routes_ref[k : k + 1, :] == experts, gates_ref[k : k + 1, :], 0.0
            )
        weight_ref[...] = weight
        sum_ref[...] = att_ref[...].astype(jnp.float32)

    span = pl.ds(pl.multiple_of(step * GROUP, GROUP), GROUP)
    slots = slot_ref[span, :]
    weights = jnp.broadcast_to(weight_ref[span, :][:, None, :], (GROUP, 8, TOK))
    weights = weights.reshape(GROUP * 8, TOK)

    def split(hit):
        value = jnp.where(hit, weights, 0.0)
        high = value.astype(jnp.bfloat16)
        low = (value - high.astype(jnp.float32)).astype(jnp.bfloat16)
        return jnp.concatenate([high, low], axis=1)

    def add_up(factors, rows):
        both = lax.dot_general(
            factors, rows, (((0,), (0,)), ((), ())), preferred_element_type=jnp.float32
        )
        return both[:TOK] + both[TOK:]

    main = split(main_slots(slots))
    packed = in_ref[:, 4].reshape(GROUP * 8, QUARTER)
    for quarter in range(4):
        part = slice(quarter * QUARTER, (quarter + 1) * QUARTER)
        rows = in_ref[:, quarter].reshape(GROUP * 8, QUARTER)
        sum_ref[:, part] += add_up(main, rows) + add_up(
            split(extra_slots(slots, quarter)), packed
        )

    @pl.when(step == pl.num_programs(0) - 1)
    def _():
        out_ref[...] = sum_ref[...].astype(jnp.bfloat16)


def combine(routes, gates, attended, messages):
    return pl.pallas_call(
        combine_kernel,
        grid=(N_DEV // GROUP,),
        out_shape=jax.ShapeDtypeStruct((TOK, D), jnp.bfloat16),
        in_specs=[
            pl.BlockSpec((8, TOK), lambda i: (0, 0)),
            pl.BlockSpec((8, TOK), lambda i: (0, 0)),
            pl.BlockSpec((TOK, D), lambda i: (0, 0)),
            pl.BlockSpec((GROUP, 5, 8, QUARTER), lambda i: (i, 0, 0, 0)),
        ],
        out_specs=pl.BlockSpec((TOK, D), lambda i: (0, 0)),
        scratch_shapes=[
            pltpu.VMEM((N_DEV, TOK), jnp.int32),
            pltpu.VMEM((N_DEV, TOK), jnp.float32),
            pltpu.VMEM((TOK, D), jnp.float32),
        ],
        compiler_params=pltpu.CompilerParams(vmem_limit_bytes=40 << 20),
        name="combine",
    )(routes, gates, attended, messages)


def local(
    query_states,
    key_states,
    value_states,
    positions,
    lengths,
    routes,
    gate_weights,
    norm_gain,
    gate_proj,
    up_proj,
    down_proj,
):
    gathered = gather_keys(key_states[0], value_states[0])
    attended, normed = attend(
        positions, lengths, query_states[0], gathered, norm_gain.reshape(1, D)
    )
    by_rank = routes[0].T
    outgoing = pack(by_rank, normed)
    arrived = exchange(outgoing, 1)
    results = expert(arrived, gate_proj[0], up_proj[0], down_proj[0])
    returned = exchange(results, 2)
    return combine(by_rank, gate_weights[0].T, attended, returned)[None]


def solution(mesh):
    in_specs = (
        P("exp", "ctx", None),
        P("exp", "ctx", None),
        P("exp", "ctx", None),
        P("exp", None),
        P("exp", None),
        P("exp", "ctx", None),
        P("exp", "ctx", None),
        P(),
        P(("ctx", "exp"), None, None),
        P(("ctx", "exp"), None, None),
        P(("ctx", "exp"), None, None),
    )
    out_specs = P("exp", "ctx", None)
    return jax.shard_map(local, mesh=mesh, in_specs=in_specs, out_specs=out_specs, check_vma=False)
```

time: 778 us -> 414 us (0.53); the launches traced: 763 us -> 414 us
  Pallas kernels: 0 us -> 404 us
  waiting for transfers between devices: 304 us -> 0 us
  blocking collectives: 195 us -> 0 us
  local copies, waits for them, and re-layouts: 120 us -> 9.72 us
  matrix products: 80.9 us -> 0 us
  other arithmetic: 43 us -> 0 us
  between operations: 14.2 us -> 0.08 us
    pallas_call x0 -> x7, Pallas kernels: none -> 404 us  [the longest x2 303 us: exchange(): pl.pallas_call(exchange_kernel, out_shape=jax.ShapeDtypeStruct(messages.s...]
    all_to_all x1 -> x0, waiting for transfers between devices: 233 us -> none  [local(): lax.all_to_all(results.reshape(sources, slots_here, width_here), ('ctx',...]
    all_to_all x1 -> x0, blocking collectives: 195 us -> none  [local(): lax.all_to_all(outgoing, ('ctx', 'exp'), split_axis=0, concat_axis=0, til...]
    dot_general x12 -> x0, matrix products: 80.9 us -> none  [the longest x4 20.5 us: online_block(): jnp.einsum('gqij,jgd->gqid', exp_terms.astype(jnp.bfloat16), value_block,...]
    all_gather x2 -> x0, waiting for transfers between devices: 69.5 us -> none  [the longest x1 42.9 us: attention_keys(): value_piece = lax.all_gather(value_states, 'ctx', axis=1, tiled=True)]
    reshape x6 -> x0, local copies, waits for them, and re-layouts: 51.1 us -> none  [the longest x1 16.7 us: local(): arrived.reshape(sources * slots_here, width_here)]
    gather x3 -> x0, local copies, waits for them, and re-layouts: 43.9 us -> none  [the longest x2 23.6 us: local(): normed[row_table]]
    reduce_sum x7 -> x0, other arithmetic: 21.9 us -> none  [the longest x4 18.6 us: online_block(): totals = totals * factor + jnp.sum(exp_terms, axis=3)]
  transfers between devices with their start and end apart: 3 -> 0, of which waited for: 3 -> 0; matrix products, arithmetic and copies ran while one was open for 3% -> 0% of each run, Pallas kernels for 0% -> 0%
where the time goes in v1:
time: 414 us
  Pallas kernels  404 us (98%)
  local copies, waits for them, and re-layouts  9.72 us (2%)
    pallas_call x2, Pallas kernels, exchange(): pl.pallas_call(exchange_kernel, out_shape=jax.ShapeDtypeStruct(messages.s...  303 us
    pallas_call x1, Pallas kernels, expert(): pl.pallas_call(expert_kernel, grid=(N_DEV // GROUP,), out_shape=jax.Shape...  38.4 us
    pallas_call x1, Pallas kernels, gather_keys(): pl.pallas_call(gather_kernel, out_shape=jax.ShapeDtypeStruct((N_CTX, 2, T...  36.5 us
    pallas_call x1, Pallas kernels, attend(): pl.pallas_call(attend_kernel, out_shape=[jax.ShapeDtypeStruct((TOK, D), j...  14.1 us
    unnamed x14, local copies, waits for them, and re-layouts  9.72 us

profile of v1, /device:TPU:32, one launch (start us, length us, event | category | flops | bytes accessed | tf_op | source)
XLA Modules:
  0.0 413.6 jit_solution(377108836750854948)
XLA Ops:
  0.0 36.5 %gather_keys.1.kv_ref = bf16[16,2,128,256]{3,2,1,0:T(8,128)(2,1)} custom-call(bf16[128,256]{1,0:T(8,128)(2,1)} %bitcast.21, bf16[128,256]{1,0:T(8,128)(2,1)} %bitcast.22), custom_call_target="tpu_custom_call" | custom-call | tf_op jit(solution)/shard_map/gather_keys/pallas_call | solution.py:79
  36.5 14.1 %attend.1 = (bf16[128,4096]{1,0:T(8,128)(2,1)}, bf16[128,4096]{1,0:T(8,128)(2,1)}) custom-call(s32[1,2048]{1,0:T(1,128)} %pos_ref.1, s32[1,16]{1,0:T(1,128)} %len_ref.1, bf16[128,4096]{1,0:T(8,128)(2,1)} %bitcast.20, bf16[16,2,128,256]{3,2,1,0:T(8,128)(2,1)} %gather_keys.1.kv_ref, f32[1,4096]{1,0:T(1,128)} %bitcast.23), custom_call_target="tpu_custom_call" | custom-call | tf_op jit(solution)/shard_map/attend/pallas_call | solution.py:163
  50.6 0.0 copy-start.3
  50.6 1.2 copy-done.3
  51.8 0.0 copy-start.4
  51.9 0.7 copy-done.4
  52.5 5.2 %pack_rows.1.in_ref = bf16[128,5,8,1024]{3,2,1,0:T(8,128)(2,1)S(1)} custom-call(s32[8,128]{1,0:T(8,128)S(1)} %bitcast.14, bf16[128,4096]{1,0:T(8,128)(2,1)S(1)} %copy-done.3), custom_call_target="tpu_custom_call" | custom-call | tf_op jit(solution)/shard_map/pack_rows/pallas_call | solution.py:223
  57.7 0.0 copy-start.1
  57.7 3.8 copy-done.1
  61.5 153.0 %exchange_1.1.in_ref = bf16[128,5,8,1024]{3,2,1,0:T(8,128)(2,1)} custom-call(bf16[128,5,8,1024]{3,2,1,0:T(8,128)(2,1)} %copy-done.1), custom_call_target="tpu_custom_call" | custom-call | tf_op jit(solution)/shard_map/exchange_1/pallas_call | solution.py:281
  214.5 38.4 %expert.1.in_ref = bf16[128,5,8,1024]{3,2,1,0:T(8,128)(2,1)} custom-call(bf16[128,5,8,1024]{3,2,1,0:T(8,128)(2,1)} %exchange_1.1.in_ref, bf16[4096,768]{1,0:T(8,128)(2,1)} %bitcast.17, bf16[4096,768]{1,0:T(8,128)(2,1)} %bitcast.18, bf16[768,4096]{1,0:T(8,128)(2,1)} %bitcast.19), custom_call_target="tpu_custom_call" | custom-call | tf_op jit(solution)/shard_map/expert/pallas_call | solution.py:335
  252.9 0.0 copy-start.2
  252.9 0.0 copy-start.5
  252.9 0.0 copy-start.6
  253.0 149.8 %exchange_2.1.in_ref = bf16[128,5,8,1024]{3,2,1,0:T(8,128)(2,1)} custom-call(bf16[128,5,8,1024]{3,2,1,0:T(8,128)(2,1)} %expert.1.in_ref), custom_call_target="tpu_custom_call" | custom-call | tf_op jit(solution)/shard_map/exchange_2/pallas_call | solution.py:281
  402.8 0.0 copy-done.2
  402.8 0.0 copy-done.5
  402.8 0.0 copy-done.6
  402.8 0.0 copy-start
  402.8 4.0 copy-done
  406.8 6.8 %combine.1 = bf16[128,4096]{1,0:T(8,128)(2,1)} custom-call(s32[8,128]{1,0:T(8,128)S(1)} %bitcast.15, f32[8,128]{1,0:T(8,128)S(1)} %bitcast.16, bf16[128,4096]{1,0:T(8,128)(2,1)S(1)} %copy-done.2, bf16[128,5,8,1024]{3,2,1,0:T(8,128)(2,1)S(1)} %copy-done), custom_call_target="tpu_custom_call" | custom-call | tf_op jit(solution)/shard_map/combine/pallas_call | solution.py:398
Async XLA Ops:
  50.6 1.2 copy-start.3
  51.8 0.7 copy-start.4
  57.7 3.8 copy-start.1
  252.9 149.9 %copy-start.2 = (bf16[128,4096]{1,0:T(8,128)(2,1)S(1)}, bf16[128,4096]{1,0:T(8,128)(2,1)}, u32[]{:S(2)}) copy-start(bf16[128,4096]{1,0:T(8,128)(2,1)} %get-tuple-element.7.att_ref) | copy-start | bytes 3145732
  252.9 149.9 %copy-start.5 = (s32[1,128,8]{1,2,0:T(8,128)S(1)}, s32[1,128,8]{1,2,0:T(8,128)}, u32[]{:S(2)}) copy-start(s32[1,128,8]{1,2,0:T(8,128)} %param.16) | copy-start | bytes 12292
  252.9 149.9 %copy-start.6 = (f32[1,128,8]{1,2,0:T(8,128)S(1)}, f32[1,128,8]{1,2,0:T(8,128)}, u32[]{:S(2)}) copy-start(f32[1,128,8]{1,2,0:T(8,128)} %param.17) | copy-start | bytes 12292
  402.8 4.0 copy-start

commit v2 on v1

v2 whole, which is shorter than its diff:
```python
import functools
import math

import jax
import jax.numpy as jnp
from jax import lax
from jax.experimental import pallas as pl
from jax.experimental.pallas import tpu as pltpu
from jax.sharding import PartitionSpec as P

QH = 32
HD = 128
D = 4096
HID = 768
TOK = 128
N_CTX = 16
N_EXP = 8
N_DEV = 128
SEQ = 2048
DOCS = 16
RUN = 64
BLOCKS = SEQ // RUN
WINDOW = 10
KEYS = WINDOW * RUN
QUARTER = D // 4
GROUP = 32
PARTS = N_DEV // GROUP
STRIDE = 91
MESH = pl.DeviceIdType.MESH

neg_large = -1e30
norm_eps = 1e-06


def peer(ctx, exp, delta):
    z, y, x, core = ctx // 4, ctx % 4, exp // 2, exp % 2
    dz, dy, dx, dcore = delta // 32, (delta // 8) % 4, (delta // 2) % 4, delta % 2
    return (
        ((z + dz) % 4) * 4 + (y + dy) % 4,
        ((x + dx) % 4) * 2 + (core + dcore) % 2,
    )


def gather_kernel(k_ref, v_ref, out_ref, send_sem, recv_sem, local_sem):
    ctx = lax.axis_index("ctx")
    exp = lax.axis_index("exp")

    def along(axis, origin, step):
        oz, oy = origin // 4, origin % 4
        if axis == 0:
            return oz * 4 + (oy + step) % 4
        return ((oz + step) % 4) * 4 + oy

    barrier = pltpu.get_barrier_semaphore()
    for axis in range(2):
        for step in range(1, 4):
            pl.semaphore_signal(
                barrier, inc=1, device_id=(along(axis, ctx, step), exp), device_id_type=MESH
            )
    pl.semaphore_wait(barrier, 6)

    started = []
    for which in range(2):
        for step in range(1, 4):
            sent = pltpu.make_async_remote_copy(
                src_ref=(k_ref, v_ref)[which],
                dst_ref=out_ref.at[ctx, which],
                send_sem=send_sem.at[which, 0, step],
                recv_sem=recv_sem.at[which, 0, step],
                device_id=(along(which, ctx, step), exp),
                device_id_type=MESH,
            )
            sent.start()
            started.append(sent)

    def pass_on(which, first):
        origin = along(which, ctx, 4 - first) if first else ctx
        for step in range(1, 4):
            sent = pltpu.make_async_remote_copy(
                src_ref=out_ref.at[origin, which] if first else (k_ref, v_ref)[which],
                dst_ref=out_ref.at[origin, which],
                send_sem=send_sem.at[which, 1 + first, step],
                recv_sem=recv_sem.at[which, 1 + first, step],
                device_id=(along(1 - which, ctx, step), exp),
                device_id_type=MESH,
            )
            sent.start()
            started.append(sent)

    for which in range(2):
        pass_on(which, 0)
    own = [
        pltpu.make_async_copy(source, out_ref.at[ctx, which], local_sem.at[which])
        for which, source in enumerate((k_ref, v_ref))
    ]
    for sent in own:
        sent.start()
    for first in (1, 3, 2):
        for which in range(2):
            started[which * 3 + first - 1].wait_recv()
            pass_on(which, first)
    for index, sent in enumerate(started):
        sent.wait_send()
        if index >= 6:
            sent.wait_recv()
    for sent in own:
        sent.wait()


def gather_keys(keys, values):
    return pl.pallas_call(
        gather_kernel,
        out_shape=jax.ShapeDtypeStruct((N_CTX, 2, TOK, 256), jnp.bfloat16),
        in_specs=[pl.BlockSpec(memory_space=pltpu.VMEM)] * 2,
        out_specs=pl.BlockSpec(memory_space=pltpu.VMEM),
        scratch_shapes=[
            pltpu.SemaphoreType.DMA((2, 5, 4)),
            pltpu.SemaphoreType.DMA((2, 5, 4)),
            pltpu.SemaphoreType.DMA((2,)),
        ],
        compiler_params=pltpu.CompilerParams(collective_id=0, has_side_effects=True),
        name="gather_keys",
    )(keys, values)


def attend_kernel(
    pos_ref, len_ref, q_ref, kv_ref, gain_ref, att_ref, norm_ref, where_ref, k_win, v_win
):
    ctx = lax.axis_index("ctx")
    for block in range(BLOCKS):
        where_ref[pos_ref[0, RUN * block] // RUN] = block
    ends = []
    total = jnp.int32(0)
    for doc in range(DOCS):
        total = total + len_ref[0, doc]
        ends.append(total)

    def one_run(run, carry):
        first_block = pos_ref[0, ctx * TOK + run * RUN] // RUN
        for step in range(WINDOW):
            block = where_ref[jnp.maximum(first_block - (WINDOW - 1) + step, 0)]
            rows = pl.ds(pl.multiple_of((block % 2) * RUN, RUN), RUN)
            k_win[pl.ds(step * RUN, RUN), :] = kv_ref[block // 2, 0, rows, :]
            v_win[pl.ds(step * RUN, RUN), :] = kv_ref[block // 2, 1, rows, :]
        own = first_block * RUN + lax.broadcasted_iota(jnp.int32, (RUN, 1), 0)
        start = jnp.zeros((RUN, 1), jnp.int32)
        for end in ends:
            start = jnp.maximum(start, jnp.where(own >= end, end, 0))
        places = (first_block - (WINDOW - 1)) * RUN + lax.broadcasted_iota(
            jnp.int32, (RUN, KEYS), 1
        )
        visible = (places >= start) & (places <= own)
        tokens = pl.ds(pl.multiple_of(run * RUN, RUN), RUN)

        def four_heads(part, inner):
            group = part // 4
            lanes = pl.ds(pl.multiple_of(group * HD, HD), HD)
            queries = jnp.concatenate(
                [
                    q_ref[tokens, pl.ds(pl.multiple_of((part * 4 + i) * HD, HD), HD)]
                    for i in range(4)
                ],
                axis=0,
            )
            scores = lax.dot_general(
                queries,
                k_win[:, lanes],
                (((1,), (1,)), ((), ())),
                preferred_element_type=jnp.float32,
            )
            scores = jnp.where(visible[None], scores.reshape(4, RUN, KEYS), neg_large)
            maxima = jnp.max(scores, axis=2, keepdims=True)
            probs = jnp.exp((scores - maxima) * (1.0 / math.sqrt(HD)))
            totals = jnp.sum(probs, axis=2, keepdims=True)
            summed = jnp.dot(
                probs.reshape(4 * RUN, KEYS).astype(jnp.bfloat16),
                v_win[:, lanes],
                preferred_element_type=jnp.float32,
            )
            result = (summed.reshape(4, RUN, HD) / totals).astype(jnp.bfloat16)
            for i in range(4):
                att_ref[tokens, pl.ds(pl.multiple_of((part * 4 + i) * HD, HD), HD)] = result[i]
            return inner

        lax.fori_loop(0, QH // 4, four_heads, 0)
        wide = att_ref[tokens, :].astype(jnp.float32)
        scale = lax.rsqrt(jnp.mean(wide * wide, axis=1, keepdims=True) + norm_eps)
        norm_ref[tokens, :] = (wide * scale * gain_ref[...]).astype(jnp.bfloat16)
        return carry

    lax.fori_loop(0, TOK // RUN, one_run, 0)


def attend(positions, lengths, queries, gathered, gain):
    return pl.pallas_call(
        attend_kernel,
        out_shape=[jax.ShapeDtypeStruct((TOK, D), jnp.bfloat16)] * 2,
        in_specs=[pl.BlockSpec(memory_space=pltpu.SMEM)] * 2
        + [pl.BlockSpec(memory_space=pltpu.VMEM)] * 3,
        out_specs=[pl.BlockSpec(memory_space=pltpu.VMEM)] * 2,
        scratch_shapes=[
            pltpu.SMEM((BLOCKS,), jnp.int32),
            pltpu.VMEM((KEYS, 256), jnp.bfloat16),
            pltpu.VMEM((KEYS, 256), jnp.bfloat16),
        ],
        name="attend",
    )(positions, lengths, queries, gathered, gain)


def slots_by_expert(routes_ref):
    experts = lax.broadcasted_iota(jnp.int32, (N_DEV, TOK), 0)
    named = jnp.zeros((N_DEV, TOK), jnp.float32)
    for k in range(8):
        named = named + (routes_ref[k : k + 1, :] == experts).astype(jnp.float32)
    earlier = (
        lax.broadcasted_iota(jnp.int32, (TOK, TOK), 0)
        < lax.broadcasted_iota(jnp.int32, (TOK, TOK), 1)
    ).astype(jnp.bfloat16)
    ranks = jnp.dot(named.astype(jnp.bfloat16), earlier, preferred_element_type=jnp.float32)
    return jnp.where(named > 0.5, ranks.astype(jnp.int32), -1)


def main_slots(slots):
    wide = jnp.broadcast_to(slots[:, None, :], (GROUP, 8, TOK))
    return (wide == lax.broadcasted_iota(jnp.int32, (GROUP, 8, TOK), 1)).reshape(GROUP * 8, TOK)


def extra_slots(slots, quarter):
    wide = jnp.broadcast_to(slots[:, None, :], (GROUP, 8, TOK))
    row = lax.broadcasted_iota(jnp.int32, (GROUP, 8, TOK), 1)
    hit = (wide == 8 + row % 2) & (row // 2 == quarter)
    return hit.reshape(GROUP * 8, TOK)


def extra_pick(quarter):
    row = lax.broadcasted_iota(jnp.int32, (GROUP * 2, GROUP * 8), 0)
    column = lax.broadcasted_iota(jnp.int32, (GROUP * 2, GROUP * 8), 1)
    hit = column == (row // 2) * 8 + quarter * 2 + row % 2
    return hit.astype(jnp.float32).astype(jnp.bfloat16)


def spans(quarter):
    return slice(quarter * QUARTER, (quarter + 1) * QUARTER)


def moe_kernel(
    routes_ref,
    gates_ref,
    att_ref,
    norm_ref,
    gate_hbm,
    up_hbm,
    down_hbm,
    out_ref,
    arrived,
    returned,
    gate_ref,
    up_ref,
    down_ref,
    messages,
    stage,
    slot_ref,
    weight_ref,
    slot_part,
    weight_part,
    sum_ref,
    send_out,
    recv_out,
    send_back,
    recv_back,
    local_sem,
):
    ctx = lax.axis_index("ctx")
    exp = lax.axis_index("exp")

    loads = [
        pltpu.make_async_copy(source, target, local_sem.at[i])
        for i, (source, target) in enumerate(
            ((gate_hbm, gate_ref), (up_hbm, up_ref), (down_hbm, down_ref))
        )
    ]
    for load in loads:
        load.start()

    barrier = pltpu.get_barrier_semaphore()

    def greet(delta, carry):
        pl.semaphore_signal(
            barrier, inc=1, device_id=peer(ctx, exp, delta), device_id_type=MESH
        )
        return carry

    lax.fori_loop(1, N_DEV, greet, 0)

    slot_ref[...] = slots_by_expert(routes_ref)
    experts = lax.broadcasted_iota(jnp.int32, (N_DEV, TOK), 0)
    weight = jnp.zeros((N_DEV, TOK), jnp.float32)
    for k in range(8):
        weight = weight + jnp.where(
            routes_ref[k : k + 1, :] == experts, gates_ref[k : k + 1, :], 0.0
        )
    weight_ref[...] = weight
    sum_ref[...] = att_ref[...].astype(jnp.float32)

    def outward(i):
        delta = (i * STRIDE) % N_DEV
        return pltpu.make_async_remote_copy(
            src_ref=messages.at[i],
            dst_ref=arrived.at[i],
            send_sem=send_out.at[i],
            recv_sem=recv_out.at[i],
            device_id=peer(ctx, exp, delta),
            device_id_type=MESH,
        )

    def homeward(i):
        delta = (i * STRIDE) % N_DEV
        dz, dy, dx, dcore = delta // 32, (delta // 8) % 4, (delta // 2) % 4, delta % 2
        back = ((4 - dz) % 4) * 32 + ((4 - dy) % 4) * 8 + ((4 - dx) % 4) * 2 + dcore
        return pltpu.make_async_remote_copy(
            src_ref=messages.at[i],
            dst_ref=returned.at[i],
            send_sem=send_back.at[i],
            recv_sem=recv_back.at[i],
            device_id=peer(ctx, exp, back),
            device_id_type=MESH,
        )

    own_out = pltpu.make_async_copy(messages.at[0], arrived.at[0], local_sem.at[3])
    own_back = pltpu.make_async_copy(messages.at[0], returned.at[0], local_sem.at[4])

    def each(part, remote, own):
        def one(j, carry):
            i = part * GROUP + j

            @pl.when(i > 0)
            def _():
                remote(i)

            @pl.when(i == 0)
            def _():
                own()

            return carry

        lax.fori_loop(0, GROUP, one, 0)

    def pick_rows(part):
        def one(j, carry):
            target = peer(ctx, exp, ((part * GROUP + j) * STRIDE) % N_DEV)
            row = target[0] * N_EXP + target[1]
            slot_part[pl.ds(j, 1), :] = slot_ref[pl.ds(row, 1), :]
            weight_part[pl.ds(j, 1), :] = weight_ref[pl.ds(row, 1), :]
            return carry

        lax.fori_loop(0, GROUP, one, 0)
        return slot_part[...]

    def pack_part(part, carry):
        slots = pick_rows(part)
        span = pl.ds(part * GROUP, GROUP)
        main = main_slots(slots).astype(jnp.float32).astype(jnp.bfloat16)
        extra = jnp.zeros((GROUP * 8, QUARTER), jnp.float32)
        for quarter in range(4):
            normed = norm_ref[:, spans(quarter)]
            rows = jnp.dot(main, normed, preferred_element_type=jnp.float32)
            messages[span, quarter] = rows.astype(jnp.bfloat16).reshape(GROUP, 8, QUARTER)
            chosen = extra_slots(slots, quarter).astype(jnp.float32).astype(jnp.bfloat16)
            extra = extra + jnp.dot(chosen, normed, preferred_element_type=jnp.float32)
        messages[span, 4] = extra.astype(jnp.bfloat16).reshape(GROUP, 8, QUARTER)

        @pl.when(part == 0)
        def _():
            pl.semaphore_wait(barrier, N_DEV - 1)

        each(part, lambda i: outward(i).start(), own_out.start)
        return carry

    lax.fori_loop(0, PARTS, pack_part, 0)
    for load in loads:
        load.wait()

    def fetch(source, part):
        copy = pltpu.make_async_copy(
            source.at[pl.ds(part * GROUP, GROUP)], stage, local_sem.at[5]
        )
        copy.start()
        copy.wait()

    def expert_part(part, carry):
        each(part, lambda i: outward(i).wait(), own_out.wait)
        fetch(arrived, part)
        span = pl.ds(part * GROUP, GROUP)
        packed = stage[:, 4].reshape(GROUP * 8, QUARTER)
        gate = jnp.zeros((GROUP * 10, HID), jnp.float32)
        up = jnp.zeros((GROUP * 10, HID), jnp.float32)
        for quarter in range(4):
            extra = jnp.dot(extra_pick(quarter), packed, preferred_element_type=jnp.float32)
            rows = jnp.concatenate(
                [stage[:, quarter].reshape(GROUP * 8, QUARTER), extra.astype(jnp.bfloat16)],
                axis=0,
            )
            gate = gate + jnp.dot(
                rows, gate_ref[spans(quarter), :], preferred_element_type=jnp.float32
            )
            up = up + jnp.dot(
                rows, up_ref[spans(quarter), :], preferred_element_type=jnp.float32
            )
        hidden = (gate / (1.0 + jnp.exp(-gate)) * up).astype(jnp.bfloat16)
        spread = jnp.zeros((GROUP * 8, QUARTER), jnp.float32)
        for quarter in range(4):
            result = jnp.dot(
                hidden, down_ref[:, spans(quarter)], preferred_element_type=jnp.float32
            ).astype(jnp.bfloat16)
            messages[span, quarter] = result[: GROUP * 8].reshape(GROUP, 8, QUARTER)
            spread = spread + lax.dot_general(
                extra_pick(quarter),
                result[GROUP * 8 :],
                (((0,), (0,)), ((), ())),
                preferred_element_type=jnp.float32,
            )
        messages[span, 4] = spread.astype(jnp.bfloat16).reshape(GROUP, 8, QUARTER)
        each(part, lambda i: homeward(i).start(), own_back.start)
        return carry

    lax.fori_loop(0, PARTS, expert_part, 0)

    def add_up(factors, rows):
        both = lax.dot_general(
            factors, rows, (((0,), (0,)), ((), ())), preferred_element_type=jnp.float32
        )
        return both[:TOK] + both[TOK:]

    def combine_part(part, carry):
        slots = pick_rows(part)
        weights = jnp.broadcast_to(weight_part[...][:, None, :], (GROUP, 8, TOK))
        weights = weights.reshape(GROUP * 8, TOK)

        def split(hit):
            value = jnp.where(hit, weights, 0.0)
            high = value.astype(jnp.bfloat16)
            low = (value - high.astype(jnp.float32)).astype(jnp.bfloat16)
            return jnp.concatenate([high, low], axis=1)

        each(part, lambda i: homeward(i).wait(), own_back.wait)
        fetch(returned, part)
        main = split(main_slots(slots))
        packed = stage[:, 4].reshape(GROUP * 8, QUARTER)
        for quarter in range(4):
            rows = stage[:, quarter].reshape(GROUP * 8, QUARTER)
            sum_ref[:, spans(quarter)] += add_up(main, rows) + add_up(
                split(extra_slots(slots, quarter)), packed
            )
        return carry

    lax.fori_loop(0, PARTS, combine_part, 0)
    out_ref[...] = sum_ref[...].astype(jnp.bfloat16)


def moe(routes, gates, attended, normed, gate, up, down):
    wire = (N_DEV, 5, 8, QUARTER)
    vmem = pl.BlockSpec(memory_space=pltpu.VMEM)
    hbm = pl.BlockSpec(memory_space=pltpu.HBM)
    return pl.pallas_call(
        moe_kernel,
        out_shape=[
            jax.ShapeDtypeStruct((TOK, D), jnp.bfloat16),
            jax.ShapeDtypeStruct(wire, jnp.bfloat16),
            jax.ShapeDtypeStruct(wire, jnp.bfloat16),
        ],
        in_specs=[vmem] * 4 + [hbm] * 3,
        out_specs=[vmem, hbm, hbm],
        scratch_shapes=[
            pltpu.VMEM((D, HID), jnp.bfloat16),
            pltpu.VMEM((D, HID), jnp.bfloat16),
            pltpu.VMEM((HID, D), jnp.bfloat16),
            pltpu.VMEM(wire, jnp.bfloat16),
            pltpu.VMEM((GROUP, 5, 8, QUARTER), jnp.bfloat16),
            pltpu.VMEM((N_DEV, TOK), jnp.int32),
            pltpu.VMEM((N_DEV, TOK), jnp.float32),
            pltpu.VMEM((GROUP, TOK), jnp.int32),
            pltpu.VMEM((GROUP, TOK), jnp.float32),
            pltpu.VMEM((TOK, D), jnp.float32),
            pltpu.SemaphoreType.DMA((N_DEV,)),
            pltpu.SemaphoreType.DMA((N_DEV,)),
            pltpu.SemaphoreType.DMA((N_DEV,)),
            pltpu.SemaphoreType.DMA((N_DEV,)),
            pltpu.SemaphoreType.DMA((6,)),
        ],
        compiler_params=pltpu.CompilerParams(
            collective_id=1, has_side_effects=True, vmem_limit_bytes=58 << 20
        ),
        name="moe",
    )(routes, gates, attended, normed, gate, up, down)[0]


def local(
    query_states,
    key_states,
    value_states,
    positions,
    lengths,
    routes,
    gate_weights,
    norm_gain,
    gate_proj,
    up_proj,
    down_proj,
):
    gathered = gather_keys(key_states[0], value_states[0])
    attended, normed = attend(
        positions, lengths, query_states[0], gathered, norm_gain.reshape(1, D)
    )
    out = moe(
        routes[0].T,
        gate_weights[0].T,
        attended,
        normed,
        gate_proj[0],
        up_proj[0],
        down_proj[0],
    )
    return out[None]


def solution(mesh):
    in_specs = (
        P("exp", "ctx", None),
        P("exp", "ctx", None),
        P("exp", "ctx", None),
        P("exp", None),
        P("exp", None),
        P("exp", "ctx", None),
        P("exp", "ctx", None),
        P(),
        P(("ctx", "exp"), None, None),
        P(("ctx", "exp"), None, None),
        P(("ctx", "exp"), None, None),
    )
    out_specs = P("exp", "ctx", None)
    return jax.shard_map(local, mesh=mesh, in_specs=in_specs, out_specs=out_specs, check_vma=False)
```

time: 414 us -> 339 us (0.82)
  Pallas kernels: 404 us -> 333 us
  local copies, waits for them, and re-layouts: 9.72 us -> 2.29 us
    pallas_call x5 -> x1, Pallas kernels: 353 us -> 296 us  [moe(): pl.pallas_call(moe_kernel, out_shape=[jax.ShapeDtypeStruct((TOK, D), jnp....]
    pallas_call x1, Pallas kernels: 36.5 us -> 23.6 us  [gather_keys(): pl.pallas_call(gather_kernel, out_shape=jax.ShapeDtypeStruct((N_CTX, 2, T...]
    unnamed x14 -> x1, local copies, waits for them, and re-layouts: 9.72 us -> 2.29 us
where the time goes in v2:
time: 339 us; the launch traced here: 336 us
  Pallas kernels  333 us (98%)
    pallas_call x1, Pallas kernels, moe(): pl.pallas_call(moe_kernel, out_shape=[jax.ShapeDtypeStruct((TOK, D), jnp....  296 us
    pallas_call x1, Pallas kernels, gather_keys(): pl.pallas_call(gather_kernel, out_shape=jax.ShapeDtypeStruct((N_CTX, 2, T...  23.6 us
    pallas_call x1, Pallas kernels, attend(): pl.pallas_call(attend_kernel, out_shape=[jax.ShapeDtypeStruct((TOK, D), j...  14.1 us

profile of v2, /device:TPU:32, one launch (start us, length us, event | category | flops | bytes accessed | tf_op | source)
XLA Modules:
  0.0 335.6 jit_solution(8125829977133201457)
XLA Ops:
  0.0 23.6 %gather_keys.1.kv_ref = bf16[16,2,128,256]{3,2,1,0:T(8,128)(2,1)} custom-call(bf16[128,256]{1,0:T(8,128)(2,1)} %bitcast.19, bf16[128,256]{1,0:T(8,128)(2,1)} %bitcast.20), custom_call_target="tpu_custom_call" | custom-call | tf_op jit(solution)/shard_map/gather_keys/pallas_call | solution.py:111
  23.6 14.1 %attend.1 = (bf16[128,4096]{1,0:T(8,128)(2,1)}, bf16[128,4096]{1,0:T(8,128)(2,1)}) custom-call(s32[1,2048]{1,0:T(1,128)} %pos_ref.1, s32[1,16]{1,0:T(1,128)} %len_ref.1, bf16[128,4096]{1,0:T(8,128)(2,1)} %bitcast.17, bf16[16,2,128,256]{3,2,1,0:T(8,128)(2,1)} %gather_keys.1.kv_ref, f32[1,4096]{1,0:T(1,128)} %bitcast.21), custom_call_target="tpu_custom_call" | custom-call | tf_op jit(solution)/shard_map/attend/pallas_call | solution.py:195
  37.7 295.7 %moe.1 = (bf16[128,4096]{1,0:T(8,128)(2,1)}, bf16[128,5,8,1024]{3,2,1,0:T(8,128)(2,1)}, bf16[128,5,8,1024]{3,2,1,0:T(8,128)(2,1)}) custom-call(s32[8,128]{1,0:T(8,128)} %bitcast.22, f32[8,128]{1,0:T(8,128)} %bitcast.23, bf16[128,4096]{1,0:T(8,128)(2,1)} %get-tuple-element.8.att_ref, bf16[128,4096]{1,0:T(8,128)(2,1)} %get-tuple-element.9.norm_ref, ...), custom_call_target="tpu_custom_call" | custom-call | tf_op jit(solution)/shard_map/moe/pallas_call | solution.py:464
  333.3 2.3 copy.13

commit v3 on v2

v3 whole, which is shorter than its diff:
```python
import functools
import math

import jax
import jax.numpy as jnp
from jax import lax
from jax.experimental import pallas as pl
from jax.experimental.pallas import tpu as pltpu
from jax.sharding import PartitionSpec as P

QH = 32
HD = 128
D = 4096
HID = 768
TOK = 128
N_CTX = 16
N_DEV = 128
SEQ = 2048
DOCS = 16
RUN = 64
BLOCKS = SEQ // RUN
WINDOW = 10
KEYS = WINDOW * RUN
MESH = pl.DeviceIdType.MESH

neg_large = -1e30
norm_eps = 1e-06


def gather_kernel(k_ref, v_ref, out_ref, send_sem, recv_sem, local_sem):
    ctx = lax.axis_index("ctx")
    exp = lax.axis_index("exp")

    def along(axis, origin, step):
        oz, oy = origin // 4, origin % 4
        if axis == 0:
            return oz * 4 + (oy + step) % 4
        return ((oz + step) % 4) * 4 + oy

    barrier = pltpu.get_barrier_semaphore()
    for axis in range(2):
        for step in range(1, 4):
            pl.semaphore_signal(
                barrier, inc=1, device_id=(along(axis, ctx, step), exp), device_id_type=MESH
            )
    pl.semaphore_wait(barrier, 6)

    started = []
    for which in range(2):
        for step in range(1, 4):
            sent = pltpu.make_async_remote_copy(
                src_ref=(k_ref, v_ref)[which],
                dst_ref=out_ref.at[ctx, which],
                send_sem=send_sem.at[which, 0, step],
                recv_sem=recv_sem.at[which, 0, step],
                device_id=(along(which, ctx, step), exp),
                device_id_type=MESH,
            )
            sent.start()
            started.append(sent)

    def pass_on(which, first):
        origin = along(which, ctx, 4 - first) if first else ctx
        for step in range(1, 4):
            sent = pltpu.make_async_remote_copy(
                src_ref=out_ref.at[origin, which] if first else (k_ref, v_ref)[which],
                dst_ref=out_ref.at[origin, which],
                send_sem=send_sem.at[which, 1 + first, step],
                recv_sem=recv_sem.at[which, 1 + first, step],
                device_id=(along(1 - which, ctx, step), exp),
                device_id_type=MESH,
            )
            sent.start()
            started.append(sent)

    for which in range(2):
        pass_on(which, 0)
    own = [
        pltpu.make_async_copy(source, out_ref.at[ctx, which], local_sem.at[which])
        for which, source in enumerate((k_ref, v_ref))
    ]
    for sent in own:
        sent.start()
    for first in (1, 3, 2):
        for which in range(2):
            started[which * 3 + first - 1].wait_recv()
            pass_on(which, first)
    for index, sent in enumerate(started):
        sent.wait_send()
        if index >= 6:
            sent.wait_recv()
    for sent in own:
        sent.wait()


def gather_keys(keys, values):
    return pl.pallas_call(
        gather_kernel,
        out_shape=jax.ShapeDtypeStruct((N_CTX, 2, TOK, 256), jnp.bfloat16),
        in_specs=[pl.BlockSpec(memory_space=pltpu.VMEM)] * 2,
        out_specs=pl.BlockSpec(memory_space=pltpu.VMEM),
        scratch_shapes=[
            pltpu.SemaphoreType.DMA((2, 5, 4)),
            pltpu.SemaphoreType.DMA((2, 5, 4)),
            pltpu.SemaphoreType.DMA((2,)),
        ],
        compiler_params=pltpu.CompilerParams(collective_id=0, has_side_effects=True),
        name="gather_keys",
    )(keys, values)


def attend_kernel(
    pos_ref, len_ref, q_ref, kv_ref, gain_ref, att_ref, norm_ref, where_ref, k_win, v_win
):
    ctx = lax.axis_index("ctx")
    for block in range(BLOCKS):
        where_ref[pos_ref[0, RUN * block] // RUN] = block
    ends = []
    total = jnp.int32(0)
    for doc in range(DOCS):
        total = total + len_ref[0, doc]
        ends.append(total)

    def one_run(run, carry):
        first_block = pos_ref[0, ctx * TOK + run * RUN] // RUN
        for step in range(WINDOW):
            block = where_ref[jnp.maximum(first_block - (WINDOW - 1) + step, 0)]
            rows = pl.ds(pl.multiple_of((block % 2) * RUN, RUN), RUN)
            k_win[pl.ds(step * RUN, RUN), :] = kv_ref[block // 2, 0, rows, :]
            v_win[pl.ds(step * RUN, RUN), :] = kv_ref[block // 2, 1, rows, :]
        own = first_block * RUN + lax.broadcasted_iota(jnp.int32, (RUN, 1), 0)
        start = jnp.zeros((RUN, 1), jnp.int32)
        for end in ends:
            start = jnp.maximum(start, jnp.where(own >= end, end, 0))
        places = (first_block - (WINDOW - 1)) * RUN + lax.broadcasted_iota(
            jnp.int32, (RUN, KEYS), 1
        )
        visible = (places >= start) & (places <= own)
        tokens = pl.ds(pl.multiple_of(run * RUN, RUN), RUN)

        def four_heads(part, inner):
            group = part // 4
            lanes = pl.ds(pl.multiple_of(group * HD, HD), HD)
            queries = jnp.concatenate(
                [
                    q_ref[tokens, pl.ds(pl.multiple_of((part * 4 + i) * HD, HD), HD)]
                    for i in range(4)
                ],
                axis=0,
            )
            scores = lax.dot_general(
                queries,
                k_win[:, lanes],
                (((1,), (1,)), ((), ())),
                preferred_element_type=jnp.float32,
            )
            scores = jnp.where(visible[None], scores.reshape(4, RUN, KEYS), neg_large)
            maxima = jnp.max(scores, axis=2, keepdims=True)
            probs = jnp.exp((scores - maxima) * (1.0 / math.sqrt(HD)))
            totals = jnp.sum(probs, axis=2, keepdims=True)
            summed = jnp.dot(
                probs.reshape(4 * RUN, KEYS).astype(jnp.bfloat16),
                v_win[:, lanes],
                preferred_element_type=jnp.float32,
            )
            result = (summed.reshape(4, RUN, HD) / totals).astype(jnp.bfloat16)
            for i in range(4):
                att_ref[tokens, pl.ds(pl.multiple_of((part * 4 + i) * HD, HD), HD)] = result[i]
            return inner

        lax.fori_loop(0, QH // 4, four_heads, 0)
        wide = att_ref[tokens, :].astype(jnp.float32)
        scale = lax.rsqrt(jnp.mean(wide * wide, axis=1, keepdims=True) + norm_eps)
        norm_ref[tokens, :] = (wide * scale * gain_ref[...]).astype(jnp.bfloat16)
        return carry

    lax.fori_loop(0, TOK // RUN, one_run, 0)


def attend(positions, lengths, queries, gathered, gain):
    return pl.pallas_call(
        attend_kernel,
        out_shape=[jax.ShapeDtypeStruct((TOK, D), jnp.bfloat16)] * 2,
        in_specs=[pl.BlockSpec(memory_space=pltpu.SMEM)] * 2
        + [pl.BlockSpec(memory_space=pltpu.VMEM)] * 3,
        out_specs=[pl.BlockSpec(memory_space=pltpu.VMEM)] * 2,
        scratch_shapes=[
            pltpu.SMEM((BLOCKS,), jnp.int32),
            pltpu.VMEM((KEYS, 256), jnp.bfloat16),
            pltpu.VMEM((KEYS, 256), jnp.bfloat16),
        ],
        name="attend",
    )(positions, lengths, queries, gathered, gain)


CUTS = ((2, (0, 1), 0, 1536), (1, (0, 2), 1536, 1280), (0, (1, 2), 2816, 1280))
WIDEST = 1536
PLANE = 32
HALF = 16


def shift(ctx, exp, steps):
    dz, dy, dx, dcore = steps
    return (
        ((ctx // 4 + dz) % 4) * 4 + (ctx % 4 + dy) % 4,
        ((exp // 2 + dx) % 4) * 2 + (exp % 2 + dcore) % 2,
    )


def line_steps(axis, step):
    steps = [0, 0, 0, 0]
    steps[axis] = step
    return steps


def plane_steps(plane, slot, sign):
    steps = [0, 0, 0, slot // HALF]
    for axis, step in zip(plane, ((slot // 4) % 4, slot % 4)):
        steps[axis] = step if sign > 0 else (4 - step) % 4
    return steps


def ones(hit):
    return hit.astype(jnp.float32).astype(jnp.bfloat16)


def main_hits(slots, count):
    wide = jnp.broadcast_to(slots[:, None, :], (count, 8, TOK))
    return (wide == lax.broadcasted_iota(jnp.int32, (count, 8, TOK), 1)).reshape(count * 8, TOK)


def extra_hits(slots, count, source):
    wide = jnp.broadcast_to(slots[:, None, :], (count, 8, TOK))
    row = lax.broadcasted_iota(jnp.int32, (count, 8, TOK), 1)
    hit = (wide == 8 + row % 2) & (row // 2 == source)
    return hit.reshape(count * 8, TOK)


def extra_order_y():
    row = lax.broadcasted_iota(jnp.int32, (64, 64), 0)
    column = lax.broadcasted_iota(jnp.int32, (64, 64), 1)
    z, y, x, i = row // 32, (row // 8) % 4, (row // 2) % 4, row % 2
    return ones(column == z * 32 + x * 8 + y * 2 + i)


def extra_order_z(half):
    row = lax.broadcasted_iota(jnp.int32, (64, 128), 0)
    column = lax.broadcasted_iota(jnp.int32, (64, 128), 1)
    z, y, x, i = row // 32 + 2 * half, (row // 8) % 4, (row // 2) % 4, row % 2
    return ones(column == (y * 4 + x) * 8 + z * 2 + i)


def moe_kernel(
    routes_ref,
    gates_ref,
    att_ref,
    norm_ref,
    gate_hbm,
    up_hbm,
    down_hbm,
    out_ref,
    arrived_0,
    arrived_1,
    arrived_2,
    returned_0,
    returned_1,
    returned_2,
    gate_ref,
    up_ref,
    down_ref,
    message_0,
    message_1,
    message_2,
    stage_0,
    stage_1,
    stage_2,
    shared_0,
    shared_1,
    shared_2,
    collect_0,
    collect_1,
    collect_2,
    all_routes,
    all_gates,
    slot_ref,
    weight_ref,
    part_sum,
    sum_ref,
    line_send,
    line_recv,
    send_out,
    recv_out,
    send_back,
    recv_back,
    local_sem,
):
    arrived = (arrived_0, arrived_1, arrived_2)
    returned = (returned_0, returned_1, returned_2)
    message = (message_0, message_1, message_2)
    stage = (stage_0, stage_1, stage_2)
    shared = (shared_0, shared_1, shared_2)
    collect = (collect_0, collect_1, collect_2)
    ctx = lax.axis_index("ctx")
    exp = lax.axis_index("exp")
    place = (ctx // 4, ctx % 4, exp // 2)
    core = exp % 2

    loads = [
        pltpu.make_async_copy(source, target, local_sem.at[i])
        for i, (source, target) in enumerate(
            ((gate_hbm, gate_ref), (up_hbm, up_ref), (down_hbm, down_ref))
        )
    ]

    barrier = pltpu.get_barrier_semaphore()

    def greet(delta, carry):
        dz, dy, dx, dcore = delta // 32, (delta // 8) % 4, (delta // 2) % 4, delta % 2

        @pl.when(dz * dy * dx == 0)
        def _():
            pl.semaphore_signal(
                barrier,
                inc=1,
                device_id=shift(ctx, exp, (dz, dy, dx, dcore)),
                device_id_type=MESH,
            )

        return carry

    lax.fori_loop(1, N_DEV, greet, 0)

    for cut, (axis, plane, first, width) in enumerate(CUTS):
        shared[cut][0] = norm_ref[:, first : first + width]
        all_routes[cut, 0] = routes_ref[...]
        all_gates[cut, 0] = gates_ref[...]
    sum_ref[...] = att_ref[...].astype(jnp.float32)
    pl.semaphore_wait(barrier, 2 * (64 - 27) - 1)

    def line_copy(cut, kind, step):
        ref = (all_routes.at[cut], all_gates.at[cut], shared[cut])[kind]
        return pltpu.make_async_remote_copy(
            src_ref=ref.at[0],
            dst_ref=ref.at[step],
            send_sem=line_send.at[cut, kind, step],
            recv_sem=line_recv.at[cut, kind, step],
            device_id=shift(ctx, exp, line_steps(CUTS[cut][0], step)),
            device_id_type=MESH,
        )

    line_copies = [
        (cut, kind, step) for kind in range(3) for step in (1, 3, 2) for cut in range(3)
    ]
    for which in line_copies:
        line_copy(*which).start()
    for load in loads:
        load.start()

    earlier = ones(
        lax.broadcasted_iota(jnp.int32, (TOK, TOK), 0)
        < lax.broadcasted_iota(jnp.int32, (TOK, TOK), 1)
    )
    for cut, (axis, plane, first, width) in enumerate(CUTS):
        for step in (1, 3, 2):
            line_copy(cut, 0, step).wait()
            line_copy(cut, 1, step).wait()
        slot = lax.broadcasted_iota(jnp.int32, (PLANE, TOK), 0)
        at = [jnp.full((PLANE, TOK), 0, jnp.int32) + coordinate for coordinate in place]
        at[plane[0]] = (at[plane[0]] + (slot // 4) % 4) % 4
        at[plane[1]] = (at[plane[1]] + slot % 4) % 4
        ids = (at[0] * 4 + at[1]) * 8 + at[2] * 2 + (core + slot // HALF) % 2

        def tables(source, carry, cut=cut, ids=ids):
            named = jnp.zeros((PLANE, TOK), jnp.float32)
            weight = jnp.zeros((PLANE, TOK), jnp.float32)
            for k in range(8):
                hit = all_routes[cut, source, k : k + 1, :] == ids
                named = named + hit.astype(jnp.float32)
                weight = weight + jnp.where(hit, all_gates[cut, source, k : k + 1, :], 0.0)
            ranks = jnp.dot(
                named.astype(jnp.bfloat16), earlier, preferred_element_type=jnp.float32
            )
            slot_ref[cut, source] = jnp.where(named > 0.5, ranks.astype(jnp.int32), -1)
            weight_ref[cut, source] = weight
            return carry

        lax.fori_loop(0, 4, tables, 0)

    for cut, (axis, plane, first, width) in enumerate(CUTS):
        for step in (1, 3, 2):
            line_copy(cut, 2, step).wait()
        extra = jnp.zeros((PLANE * 8, width), jnp.float32)
        for source in range(4):
            slots = slot_ref[cut, source]
            tokens = shared[cut][source]
            rows = jnp.dot(
                ones(main_hits(slots, PLANE)), tokens, preferred_element_type=jnp.float32
            )
            message[cut][:, source] = rows.astype(jnp.bfloat16).reshape(PLANE, 8, width)
            extra = extra + jnp.dot(
                ones(extra_hits(slots, PLANE, source)),
                tokens,
                preferred_element_type=jnp.float32,
            )
        message[cut][:, 4] = extra.astype(jnp.bfloat16).reshape(PLANE, 8, width)

    def outward(cut, slot):
        return pltpu.make_async_remote_copy(
            src_ref=message[cut].at[slot],
            dst_ref=arrived[cut].at[slot],
            send_sem=send_out.at[cut, slot],
            recv_sem=recv_out.at[cut, slot],
            device_id=shift(ctx, exp, plane_steps(CUTS[cut][1], slot, 1)),
            device_id_type=MESH,
        )

    def homeward(cut, slot):
        return pltpu.make_async_remote_copy(
            src_ref=message[cut].at[slot],
            dst_ref=returned[cut].at[slot],
            send_sem=send_back.at[cut, slot],
            recv_sem=recv_back.at[cut, slot],
            device_id=shift(ctx, exp, plane_steps(CUTS[cut][1], slot, -1)),
            device_id_type=MESH,
        )

    def own_copy(cut, target, sem):
        return pltpu.make_async_copy(message[cut].at[0], target[cut].at[0], local_sem.at[sem])

    def own_out(cut):
        return own_copy(cut, arrived, 3 + cut)

    def own_back(cut):
        return own_copy(cut, returned, 6 + cut)

    def each(half, cuts, remote, own):
        def one(k, carry):
            slot = half * HALF + (k * 7) % HALF

            @pl.when(slot > 0)
            def _():
                for cut in cuts:
                    remote(cut, slot)

            @pl.when(slot == 0)
            def _():
                for cut in cuts:
                    own(cut)

            return carry

        lax.fori_loop(0, HALF, one, 0)

    every = (0, 1, 2)
    for half in range(2):
        each(half, every, lambda cut, slot: outward(cut, slot).start(), lambda cut: own_out(cut).start())
    for load in loads:
        load.wait()

    def fetch(source, cut, half):
        return pltpu.make_async_copy(
            source[cut].at[pl.ds(half * HALF, HALF)], stage[cut], local_sem.at[9 + cut]
        )

    def expert_half(half, carry):
        each(half, every, lambda cut, slot: outward(cut, slot).wait(), lambda cut: own_out(cut).wait())
        for cut in every:
            fetch(arrived, cut, half).start()
        for cut in every:
            fetch(arrived, cut, half).wait()

        def two_z(pair, inner):
            near = pl.ds(pl.multiple_of(pair * 8, 8), 8)
            order_y = extra_order_y()
            order_z = extra_order_z(pair)
            gate = jnp.zeros((320, HID), jnp.float32)
            up = jnp.zeros((320, HID), jnp.float32)
            for cut, (axis, plane, first, width) in enumerate(CUTS):
                if cut == 0:
                    pieces = [
                        stage[0][pl.ds(pair * 8 + k, 1), 0:4].reshape(32, width) for k in range(8)
                    ]
                    pieces.append(stage[0][near, 4].reshape(64, width))
                elif cut == 1:
                    pieces = [
                        stage[1][pl.ds(pair * 8 + z * 4, 4), y].reshape(32, width)
                        for z in range(2)
                        for y in range(4)
                    ]
                    packed = stage[1][near, 4].reshape(64, width)
                    extra = jnp.dot(order_y, packed, preferred_element_type=jnp.float32)
                    pieces.append(extra.astype(jnp.bfloat16))
                else:
                    pieces = [
                        stage[2][:, pair * 2 + z].reshape(128, width) for z in range(2)
                    ]
                    packed = stage[2][:, 4].reshape(128, width)
                    extra = jnp.dot(order_z, packed, preferred_element_type=jnp.float32)
                    pieces.append(extra.astype(jnp.bfloat16))
                rows = jnp.concatenate(pieces, axis=0)
                span = slice(first, first + width)
                gate = gate + jnp.dot(rows, gate_ref[span, :], preferred_element_type=jnp.float32)
                up = up + jnp.dot(rows, up_ref[span, :], preferred_element_type=jnp.float32)
            hidden = (gate / (1.0 + jnp.exp(-gate)) * up).astype(jnp.bfloat16)
            base = half * HALF
            for cut, (axis, plane, first, width) in enumerate(CUTS):
                result = jnp.dot(
                    hidden, down_ref[:, first : first + width], preferred_element_type=jnp.float32
                ).astype(jnp.bfloat16)
                last = result[256:]
                if cut == 0:
                    for k in range(8):
                        message[0][pl.ds(base + pair * 8 + k, 1), 0:4] = result[
                            k * 32 : k * 32 + 32
                        ].reshape(1, 4, 8, width)
                    message[0][pl.ds(base + pair * 8, 8), 4] = last.reshape(8, 8, width)
                elif cut == 1:
                    for z in range(2):
                        for y in range(4):
                            k = z * 4 + y
                            message[1][pl.ds(base + pair * 8 + z * 4, 4), y] = result[
                                k * 32 : k * 32 + 32
                            ].reshape(4, 8, width)
                    spread = lax.dot_general(
                        order_y, last, (((0,), (0,)), ((), ())), preferred_element_type=jnp.float32
                    )
                    message[1][pl.ds(base + pair * 8, 8), 4] = spread.astype(
                        jnp.bfloat16
                    ).reshape(8, 8, width)
                else:
                    whole = pl.ds(base, HALF)
                    for z in range(2):
                        message[2][whole, pair * 2 + z] = result[
                            z * 128 : z * 128 + 128
                        ].reshape(HALF, 8, width)
                    spread = lax.dot_general(
                        order_z, last, (((0,), (0,)), ((), ())), preferred_element_type=jnp.float32
                    ).astype(jnp.bfloat16).reshape(HALF, 8, width)
                    held = message[2][whole, 4]
                    message[2][whole, 4] = spread + jnp.where(
                        pair == 0, jnp.zeros_like(held), held
                    )
            return inner

        lax.fori_loop(0, 2, two_z, 0)
        each(half, every, lambda cut, slot: homeward(cut, slot).start(), lambda cut: own_back(cut).start())
        return carry

    lax.fori_loop(0, 2, expert_half, 0)

    def collect_copy(cut, source):
        axis = CUTS[cut][0]
        return pltpu.make_async_remote_copy(
            src_ref=shared[cut].at[source],
            dst_ref=collect[cut].at[source - 1],
            send_sem=line_send.at[cut, 3, source],
            recv_sem=line_recv.at[cut, 3, source],
            device_id=shift(ctx, exp, line_steps(axis, 4 - source)),
            device_id_type=MESH,
        )

    def answers(cut, half):
        width = CUTS[cut][3]
        each(half, (cut,), lambda c, slot: homeward(c, slot).wait(), lambda c: own_back(c).wait())
        copy = fetch(returned, cut, half)
        copy.start()
        copy.wait()

        def one(source, carry):
            span = pl.ds(half * HALF, HALF)
            slots = slot_ref[cut, source, span, :]
            weights = jnp.broadcast_to(
                weight_ref[cut, source, span, :][:, None, :], (HALF, 8, TOK)
            ).reshape(HALF * 8, TOK)
            value = jnp.concatenate(
                [
                    jnp.where(main_hits(slots, HALF), weights, 0.0),
                    jnp.where(extra_hits(slots, HALF, source), weights, 0.0),
                ],
                axis=0,
            )
            high = value.astype(jnp.bfloat16)
            low = (value - high.astype(jnp.float32)).astype(jnp.bfloat16)
            factors = jnp.concatenate([high, low], axis=1)
            rows = jnp.concatenate(
                [
                    stage[cut][:, source].reshape(HALF * 8, width),
                    stage[cut][:, 4].reshape(HALF * 8, width),
                ],
                axis=0,
            )
            both = lax.dot_general(
                factors, rows, (((0,), (0,)), ((), ())), preferred_element_type=jnp.float32
            )
            total = both[:TOK] + both[TOK:]
            if half == 0:
                part_sum[source, :, 0:width] = total
            else:
                part_sum[source, :, 0:width] = part_sum[source, :, 0:width] + total
            return carry

        lax.fori_loop(0, 4, one, 0)

    for cut, (axis, plane, first, width) in enumerate(CUTS):
        answers(cut, 0)
        answers(cut, 1)
        for source in (1, 3, 2):
            shared[cut][source] = part_sum[source, :, 0:width].astype(jnp.bfloat16)
            collect_copy(cut, source).start()
        span = slice(first, first + width)
        sum_ref[:, span] = sum_ref[:, span] + part_sum[0, :, 0:width]
    for cut, (axis, plane, first, width) in enumerate(CUTS):
        span = slice(first, first + width)
        for source in (1, 3, 2):
            collect_copy(cut, source).wait()
        total = sum_ref[:, span]
        for source in range(3):
            total = total + collect[cut][source].astype(jnp.float32)
        out_ref[:, span] = total.astype(jnp.bfloat16)


def moe(routes, gates, attended, normed, gate, up, down):
    vmem = pl.BlockSpec(memory_space=pltpu.VMEM)
    hbm = pl.BlockSpec(memory_space=pltpu.HBM)
    widths = [width for axis, plane, first, width in CUTS]
    wire = [(PLANE, 5, 8, width) for width in widths]
    return pl.pallas_call(
        moe_kernel,
        out_shape=[jax.ShapeDtypeStruct((TOK, D), jnp.bfloat16)]
        + [jax.ShapeDtypeStruct(shape, jnp.bfloat16) for shape in wire] * 2,
        in_specs=[vmem] * 4 + [hbm] * 3,
        out_specs=[vmem] + [hbm] * 6,
        scratch_shapes=[
            pltpu.VMEM((D, HID), jnp.bfloat16),
            pltpu.VMEM((D, HID), jnp.bfloat16),
            pltpu.VMEM((HID, D), jnp.bfloat16),
        ]
        + [pltpu.VMEM(shape, jnp.bfloat16) for shape in wire]
        + [pltpu.VMEM((HALF, 5, 8, width), jnp.bfloat16) for width in widths]
        + [pltpu.VMEM((4, TOK, width), jnp.bfloat16) for width in widths]
        + [pltpu.VMEM((3, TOK, width), jnp.bfloat16) for width in widths]
        + [
            pltpu.VMEM((3, 4, 8, TOK), jnp.int32),
            pltpu.VMEM((3, 4, 8, TOK), jnp.float32),
            pltpu.VMEM((3, 4, PLANE, TOK), jnp.int32),
            pltpu.VMEM((3, 4, PLANE, TOK), jnp.float32),
            pltpu.VMEM((4, TOK, WIDEST), jnp.float32),
            pltpu.VMEM((TOK, D), jnp.float32),
            pltpu.SemaphoreType.DMA((3, 4, 4)),
            pltpu.SemaphoreType.DMA((3, 4, 4)),
            pltpu.SemaphoreType.DMA((3, PLANE)),
            pltpu.SemaphoreType.DMA((3, PLANE)),
            pltpu.SemaphoreType.DMA((3, PLANE)),
            pltpu.SemaphoreType.DMA((3, PLANE)),
            pltpu.SemaphoreType.DMA((12,)),
        ],
        compiler_params=pltpu.CompilerParams(
            collective_id=1, has_side_effects=True, vmem_limit_bytes=62 << 20
        ),
        name="moe",
    )(routes, gates, attended, normed, gate, up, down)[0]


def local(
    query_states,
    key_states,
    value_states,
    positions,
    lengths,
    routes,
    gate_weights,
    norm_gain,
    gate_proj,
    up_proj,
    down_proj,
):
    gathered = gather_keys(key_states[0], value_states[0])
    attended, normed = attend(
        positions, lengths, query_states[0], gathered, norm_gain.reshape(1, D)
    )
    out = moe(
        routes[0].T,
        gate_weights[0].T,
        attended,
        normed,
        gate_proj[0],
        up_proj[0],
        down_proj[0],
    )
    return out[None]


def solution(mesh):
    in_specs = (
        P("exp", "ctx", None),
        P("exp", "ctx", None),
        P("exp", "ctx", None),
        P("exp", None),
        P("exp", None),
        P("exp", "ctx", None),
        P("exp", "ctx", None),
        P(),
        P(("ctx", "exp"), None, None),
        P(("ctx", "exp"), None, None),
        P(("ctx", "exp"), None, None),
    )
    out_specs = P("exp", "ctx", None)
    return jax.shard_map(local, mesh=mesh, in_specs=in_specs, out_specs=out_specs, check_vma=False)
```

time: 339 us -> 281 us (0.83)
  Pallas kernels: 333 us -> 276 us
    pallas_call x1, Pallas kernels: 296 us -> 238 us  [moe(): pl.pallas_call(moe_kernel, out_shape=[jax.ShapeDtypeStruct((TOK, D), jnp....]
where the time goes in v3:
time: 281 us; the launch traced here: 278 us
  Pallas kernels  276 us (98%)
    pallas_call x1, Pallas kernels, moe(): pl.pallas_call(moe_kernel, out_shape=[jax.ShapeDtypeStruct((TOK, D), jnp....  238 us
    pallas_call x1, Pallas kernels, gather_keys(): pl.pallas_call(gather_kernel, out_shape=jax.ShapeDtypeStruct((N_CTX, 2, T...  23.6 us
    pallas_call x1, Pallas kernels, attend(): pl.pallas_call(attend_kernel, out_shape=[jax.ShapeDtypeStruct((TOK, D), j...  14.1 us

profile of v3, /device:TPU:32, one launch (start us, length us, event | category | flops | bytes accessed | tf_op | source)
XLA Modules:
  0.0 278.4 jit_solution(11062334494863694889)
XLA Ops:
  0.0 23.6 %gather_keys.1.kv_ref = bf16[16,2,128,256]{3,2,1,0:T(8,128)(2,1)} custom-call(bf16[128,256]{1,0:T(8,128)(2,1)} %bitcast.19, bf16[128,256]{1,0:T(8,128)(2,1)} %bitcast.20), custom_call_target="tpu_custom_call" | custom-call | tf_op jit(solution)/shard_map/gather_keys/pallas_call | solution.py:97
  23.6 14.1 %attend.1 = (bf16[128,4096]{1,0:T(8,128)(2,1)}, bf16[128,4096]{1,0:T(8,128)(2,1)}) custom-call(s32[1,2048]{1,0:T(1,128)} %pos_ref.1, s32[1,16]{1,0:T(1,128)} %len_ref.1, bf16[128,4096]{1,0:T(8,128)(2,1)} %bitcast.17, bf16[16,2,128,256]{3,2,1,0:T(8,128)(2,1)} %gather_keys.1.kv_ref, f32[1,4096]{1,0:T(1,128)} %bitcast.21), custom_call_target="tpu_custom_call" | custom-call | tf_op jit(solution)/shard_map/attend/pallas_call | solution.py:181
  37.7 238.4 %moe.1 = (bf16[128,4096]{1,0:T(8,128)(2,1)}, bf16[32,5,8,1536]{3,2,1,0:T(8,128)(2,1)}, bf16[32,5,8,1280]{3,2,1,0:T(8,128)(2,1)}, bf16[32,5,8,1280]{3,2,1,0:T(8,1...) custom-call(s32[8,128]{1,0:T(8,128)} %bitcast.22, ...), custom_call_target="tpu_custom_call" | custom-call | tf_op jit(solution)/shard_map/moe/pallas_call | solution.py:627
  276.1 2.3 copy.13

commit v4 on v3

--- a/solution.py
+++ b/solution.py
@@ -138,37 +138,42 @@
         visible = (places >= start) & (places <= own)
         tokens = pl.ds(pl.multiple_of(run * RUN, RUN), RUN)
 
-        def four_heads(part, inner):
-            group = part // 4
-            lanes = pl.ds(pl.multiple_of(group * HD, HD), HD)
-            queries = jnp.concatenate(
-                [
-                    q_ref[tokens, pl.ds(pl.multiple_of((part * 4 + i) * HD, HD), HD)]
-                    for i in range(4)
-                ],
-                axis=0,
-            )
-            scores = lax.dot_general(
-                queries,
-                k_win[:, lanes],
-                (((1,), (1,)), ((), ())),
-                preferred_element_type=jnp.float32,
-            )
-            scores = jnp.where(visible[None], scores.reshape(4, RUN, KEYS), neg_large)
-            maxima = jnp.max(scores, axis=2, keepdims=True)
-            probs = jnp.exp((scores - maxima) * (1.0 / math.sqrt(HD)))
-            totals = jnp.sum(probs, axis=2, keepdims=True)
-            summed = jnp.dot(
-                probs.reshape(4 * RUN, KEYS).astype(jnp.bfloat16),
-                v_win[:, lanes],
-                preferred_element_type=jnp.float32,
-            )
-            result = (summed.reshape(4, RUN, HD) / totals).astype(jnp.bfloat16)
-            for i in range(4):
-                att_ref[tokens, pl.ds(pl.multiple_of((part * 4 + i) * HD, HD), HD)] = result[i]
+        def eight_heads(pair, inner):
+            chains = []
+            for part in (2 * pair, 2 * pair + 1):
+                lanes = pl.ds(pl.multiple_of((part // 4) * HD, HD), HD)
+                queries = jnp.concatenate(
+                    [
+                        q_ref[tokens, pl.ds(pl.multiple_of((part * 4 + i) * HD, HD), HD)]
+                        for i in range(4)
+                    ],
+                    axis=0,
+                )
+                scores = lax.dot_general(
+                    queries,
+                    k_win[:, lanes],
+                    (((1,), (1,)), ((), ())),
+                    preferred_element_type=jnp.float32,
+                )
+                chains.append((part, lanes, scores))
+            for part, lanes, scores in chains:
+                scores = jnp.where(visible[None], scores.reshape(4, RUN, KEYS), neg_large)
+                maxima = jnp.max(scores, axis=2, keepdims=True)
+                probs = jnp.exp((scores - maxima) * (1.0 / math.sqrt(HD)))
+                totals = jnp.sum(probs, axis=2, keepdims=True)
+                summed = jnp.dot(
+                    probs.reshape(4 * RUN, KEYS).astype(jnp.bfloat16),
+                    v_win[:, lanes],
+                    preferred_element_type=jnp.float32,
+                )
+                result = (summed.reshape(4, RUN, HD) / totals).astype(jnp.bfloat16)
+                for i in range(4):
+                    att_ref[
+                        tokens, pl.ds(pl.multiple_of((part * 4 + i) * HD, HD), HD)
+                    ] = result[i]
             return inner
 
-        lax.fori_loop(0, QH // 4, four_heads, 0)
+        lax.fori_loop(0, QH // 8, eight_heads, 0)
         wide = att_ref[tokens, :].astype(jnp.float32)
         scale = lax.rsqrt(jnp.mean(wide * wide, axis=1, keepdims=True) + norm_eps)
         norm_ref[tokens, :] = (wide * scale * gain_ref[...]).astype(jnp.bfloat16)
@@ -194,7 +199,6 @@
 
 
 CUTS = ((2, (0, 1), 0, 1536), (1, (0, 2), 1536, 1280), (0, (1, 2), 2816, 1280))
-WIDEST = 1536
 PLANE = 32
 HALF = 16
 
@@ -285,7 +289,6 @@
     slot_ref,
     weight_ref,
     part_sum,
-    sum_ref,
     line_send,
     line_recv,
     send_out,
@@ -334,7 +337,6 @@
         shared[cut][0] = norm_ref[:, first : first + width]
         all_routes[cut, 0] = routes_ref[...]
         all_gates[cut, 0] = gates_ref[...]
-    sum_ref[...] = att_ref[...].astype(jnp.float32)
     pl.semaphore_wait(barrier, 2 * (64 - 27) - 1)
 
     def line_copy(cut, kind, step):
@@ -360,49 +362,56 @@
         lax.broadcasted_iota(jnp.int32, (TOK, TOK), 0)
         < lax.broadcasted_iota(jnp.int32, (TOK, TOK), 1)
     )
-    for cut, (axis, plane, first, width) in enumerate(CUTS):
-        for step in (1, 3, 2):
-            line_copy(cut, 0, step).wait()
-            line_copy(cut, 1, step).wait()
+    def tables(cut, source):
+        plane = CUTS[cut][1]
         slot = lax.broadcasted_iota(jnp.int32, (PLANE, TOK), 0)
         at = [jnp.full((PLANE, TOK), 0, jnp.int32) + coordinate for coordinate in place]
         at[plane[0]] = (at[plane[0]] + (slot // 4) % 4) % 4
         at[plane[1]] = (at[plane[1]] + slot % 4) % 4
         ids = (at[0] * 4 + at[1]) * 8 + at[2] * 2 + (core + slot // HALF) % 2
-
-        def tables(source, carry, cut=cut, ids=ids):
-            named = jnp.zeros((PLANE, TOK), jnp.float32)
-            weight = jnp.zeros((PLANE, TOK), jnp.float32)
-            for k in range(8):
-                hit = all_routes[cut, source, k : k + 1, :] == ids
-                named = named + hit.astype(jnp.float32)
-                weight = weight + jnp.where(hit, all_gates[cut, source, k : k + 1, :], 0.0)
-            ranks = jnp.dot(
-                named.astype(jnp.bfloat16), earlier, preferred_element_type=jnp.float32
-            )
-            slot_ref[cut, source] = jnp.where(named > 0.5, ranks.astype(jnp.int32), -1)
-            weight_ref[cut, source] = weight
+        named = jnp.zeros((PLANE, TOK), jnp.float32)
+        weight = jnp.zeros((PLANE, TOK), jnp.float32)
+        for k in range(8):
+            hit = all_routes[cut, source, k : k + 1, :] == ids
+            named = named + hit.astype(jnp.float32)
+            weight = weight + jnp.where(hit, all_gates[cut, source, k : k + 1, :], 0.0)
+        ranks = jnp.dot(named.astype(jnp.bfloat16), earlier, preferred_element_type=jnp.float32)
+        slot_ref[cut, source] = jnp.where(named > 0.5, ranks.astype(jnp.int32), -1)
+        weight_ref[cut, source] = weight
+
+    def pack_main(cut, source):
+        rows = jnp.dot(
+            ones(main_hits(slot_ref[cut, source], PLANE)),
+            shared[cut][source],
+            preferred_element_type=jnp.float32,
+        )
+        message[cut][:, source] = rows.astype(jnp.bfloat16).reshape(PLANE, 8, CUTS[cut][3])
+
+    def pack_extra(cut):
+        width = CUTS[cut][3]
+        hits = jnp.concatenate(
+            [ones(extra_hits(slot_ref[cut, source], PLANE, source)) for source in range(4)], axis=1
+        )
+        rows = jnp.dot(
+            hits, shared[cut][...].reshape(4 * TOK, width), preferred_element_type=jnp.float32
+        )
+        message[cut][:, 4] = rows.astype(jnp.bfloat16).reshape(PLANE, 8, width)
+
+    def sources(cut, first, last, work):
+        def one(source, carry):
+            work(cut, source)
             return carry
 
-        lax.fori_loop(0, 4, tables, 0)
-
-    for cut, (axis, plane, first, width) in enumerate(CUTS):
+        lax.fori_loop(first, last, one, 0)
+
+    for cut in range(3):
+        tables(cut, 0)
+        pack_main(cut, 0)
+    for cut in range(3):
         for step in (1, 3, 2):
-            line_copy(cut, 2, step).wait()
-        extra = jnp.zeros((PLANE * 8, width), jnp.float32)
-        for source in range(4):
-            slots = slot_ref[cut, source]
-            tokens = shared[cut][source]
-            rows = jnp.dot(
-                ones(main_hits(slots, PLANE)), tokens, preferred_element_type=jnp.float32
-            )
-            message[cut][:, source] = rows.astype(jnp.bfloat16).reshape(PLANE, 8, width)
-            extra = extra + jnp.dot(
-                ones(extra_hits(slots, PLANE, source)),
-                tokens,
-                preferred_element_type=jnp.float32,
-            )
-        message[cut][:, 4] = extra.astype(jnp.bfloat16).reshape(PLANE, 8, width)
+            line_copy(cut, 0, step).wait()
+            line_copy(cut, 1, step).wait()
+        sources(cut, 1, 4, tables)
 
     def outward(cut, slot):
         return pltpu.make_async_remote_copy(
@@ -433,7 +442,7 @@
     def own_back(cut):
         return own_copy(cut, returned, 6 + cut)
 
-    def each(half, cuts, remote, own):
+    def each(half, cuts, remote, own, begin=0, end=HALF):
         def one(k, carry):
             slot = half * HALF + (k * 7) % HALF
 
@@ -449,11 +458,24 @@
 
             return carry
 
-        lax.fori_loop(0, HALF, one, 0)
+        lax.fori_loop(begin, end, one, 0)
 
     every = (0, 1, 2)
-    for half in range(2):
-        each(half, every, lambda cut, slot: outward(cut, slot).start(), lambda cut: own_out(cut).start())
+    def send(cut, slot):
+        outward(cut, slot).start()
+
+    def send_own(cut):
+        own_out(cut).start()
+
+    early = 4
+    for cut in every:
+        for step in (1, 3, 2):
+            line_copy(cut, 2, step).wait()
+        sources(cut, 1, 4, pack_main)
+        pack_extra(cut)
+        each(0, (cut,), send, send_own, 0, early)
+    each(0, every, send, send_own, early, HALF)
+    each(1, every, send, send_own)
     for load in loads:
         load.wait()
 
@@ -540,10 +562,27 @@
                     message[2][whole, 4] = spread + jnp.where(
                         pair == 0, jnp.zeros_like(held), held
                     )
+
+            def answer(k, inner):
+                slot = base + pair * 8 + (k * 3) % 8
+
+                @pl.when(slot > 0)
+                def _():
+                    homeward(0, slot).start()
+                    homeward(1, slot).start()
+
+                @pl.when(slot == 0)
+                def _():
+                    own_back(0).start()
+                    own_back(1).start()
+
+                return inner
+
+            lax.fori_loop(0, 8, answer, 0)
             return inner
 
         lax.fori_loop(0, 2, two_z, 0)
-        each(half, every, lambda cut, slot: homeward(cut, slot).start(), lambda cut: own_back(cut).start())
+        each(half, (2,), lambda cut, slot: homeward(cut, slot).start(), lambda cut: own_back(cut).start())
         return carry
 
     lax.fori_loop(0, 2, expert_half, 0)
@@ -560,7 +599,7 @@
         )
 
     def answers(cut, half):
-        width = CUTS[cut][3]
+        first, width = CUTS[cut][2:]
         each(half, (cut,), lambda c, slot: homeward(c, slot).wait(), lambda c: own_back(c).wait())
         copy = fetch(returned, cut, half)
         copy.start()
@@ -594,28 +633,26 @@
             )
             total = both[:TOK] + both[TOK:]
             if half == 0:
-                part_sum[source, :, 0:width] = total
+                part_sum[source, :, first : first + width] = total
             else:
-                part_sum[source, :, 0:width] = part_sum[source, :, 0:width] + total
+                part_sum[source, :, first : first + width] += total
             return carry
 
         lax.fori_loop(0, 4, one, 0)
 
+    for cut in every:
+        answers(cut, 0)
     for cut, (axis, plane, first, width) in enumerate(CUTS):
-        answers(cut, 0)
         answers(cut, 1)
         for source in (1, 3, 2):
-            shared[cut][source] = part_sum[source, :, 0:width].astype(jnp.bfloat16)
+            shared[cut][source] = part_sum[source, :, first : first + width].astype(jnp.bfloat16)
             collect_copy(cut, source).start()
-        span = slice(first, first + width)
-        sum_ref[:, span] = sum_ref[:, span] + part_sum[0, :, 0:width]
     for cut, (axis, plane, first, width) in enumerate(CUTS):
         span = slice(first, first + width)
+        total = att_ref[:, span].astype(jnp.float32) + part_sum[0, :, span]
         for source in (1, 3, 2):
             collect_copy(cut, source).wait()
-        total = sum_ref[:, span]
-        for source in range(3):
-            total = total + collect[cut][source].astype(jnp.float32)
+            total = total + collect[cut][source - 1].astype(jnp.float32)
         out_ref[:, span] = total.astype(jnp.bfloat16)
 
 
@@ -644,8 +681,7 @@
             pltpu.VMEM((3, 4, 8, TOK), jnp.float32),
             pltpu.VMEM((3, 4, PLANE, TOK), jnp.int32),
             pltpu.VMEM((3, 4, PLANE, TOK), jnp.float32),
-            pltpu.VMEM((4, TOK, WIDEST), jnp.float32),
-            pltpu.VMEM((TOK, D), jnp.float32),
+            pltpu.VMEM((4, TOK, D), jnp.float32),
             pltpu.SemaphoreType.DMA((3, 4, 4)),
             pltpu.SemaphoreType.DMA((3, 4, 4)),
             pltpu.SemaphoreType.DMA((3, PLANE)),

time: 281 us -> 274 us (0.975)
  Pallas kernels: 276 us -> 267 us
    pallas_call x1, Pallas kernels: 238 us -> 233 us  [moe(): pl.pallas_call(moe_kernel, out_shape=[jax.ShapeDtypeStruct((TOK, D), jnp....]
    pallas_call x1, Pallas kernels: 14.1 us -> 10.6 us  [attend(): pl.pallas_call(attend_kernel, out_shape=[jax.ShapeDtypeStruct((TOK, D), j...]
where the time goes in v4:
time: 274 us; the launch traced here: 269 us
  Pallas kernels  267 us (97%)
    pallas_call x1, Pallas kernels, moe(): pl.pallas_call(moe_kernel, out_shape=[jax.ShapeDtypeStruct((TOK, D), jnp....  233 us
    pallas_call x1, Pallas kernels, gather_keys(): pl.pallas_call(gather_kernel, out_shape=jax.ShapeDtypeStruct((N_CTX, 2, T...  23.6 us
    pallas_call x1, Pallas kernels, attend(): pl.pallas_call(attend_kernel, out_shape=[jax.ShapeDtypeStruct((TOK, D), j...  10.6 us

profile of v4, /device:TPU:32, one launch (start us, length us, event | category | flops | bytes accessed | tf_op | source)
XLA Modules:
  0.0 269.3 jit_solution(15883944815241570010)
XLA Ops:
  0.0 23.6 %gather_keys.1.kv_ref = bf16[16,2,128,256]{3,2,1,0:T(8,128)(2,1)} custom-call(bf16[128,256]{1,0:T(8,128)(2,1)} %bitcast.19, bf16[128,256]{1,0:T(8,128)(2,1)} %bitcast.20), custom_call_target="tpu_custom_call" | custom-call | tf_op jit(solution)/shard_map/gather_keys/pallas_call | solution.py:97
  23.6 10.6 %attend.1 = (bf16[128,4096]{1,0:T(8,128)(2,1)}, bf16[128,4096]{1,0:T(8,128)(2,1)}) custom-call(s32[1,2048]{1,0:T(1,128)} %pos_ref.1, s32[1,16]{1,0:T(1,128)} %len_ref.1, bf16[128,4096]{1,0:T(8,128)(2,1)} %bitcast.17, bf16[16,2,128,256]{3,2,1,0:T(8,128)(2,1)} %gather_keys.1.kv_ref, f32[1,4096]{1,0:T(1,128)} %bitcast.21), custom_call_target="tpu_custom_call" | custom-call | tf_op jit(solution)/shard_map/attend/pallas_call | solution.py:186
  34.2 232.8 %moe.1 = (bf16[128,4096]{1,0:T(8,128)(2,1)}, bf16[32,5,8,1536]{3,2,1,0:T(8,128)(2,1)}, bf16[32,5,8,1280]{3,2,1,0:T(8,128)(2,1)}, bf16[32,5,8,1280]{3,2,1,0:T(8,1...) custom-call(s32[8,128]{1,0:T(8,128)} %bitcast.22, ...), custom_call_target="tpu_custom_call" | custom-call | tf_op jit(solution)/shard_map/moe/pallas_call | solution.py:664
  267.0 2.3 copy.13

commit v5 on v4

--- a/solution.py
+++ b/solution.py
@@ -27,7 +27,8 @@
 norm_eps = 1e-06
 
 
-def gather_kernel(k_ref, v_ref, out_ref, send_sem, recv_sem, local_sem):
+def gather_kernel(k_ref, v_ref, all_k, all_v, send_sem, recv_sem, local_sem):
+    out = (all_k, all_v)
     ctx = lax.axis_index("ctx")
     exp = lax.axis_index("exp")
 
@@ -50,7 +51,7 @@
         for step in range(1, 4):
             sent = pltpu.make_async_remote_copy(
                 src_ref=(k_ref, v_ref)[which],
-                dst_ref=out_ref.at[ctx, which],
+                dst_ref=out[which].at[ctx],
                 send_sem=send_sem.at[which, 0, step],
                 recv_sem=recv_sem.at[which, 0, step],
                 device_id=(along(which, ctx, step), exp),
@@ -63,8 +64,8 @@
         origin = along(which, ctx, 4 - first) if first else ctx
         for step in range(1, 4):
             sent = pltpu.make_async_remote_copy(
-                src_ref=out_ref.at[origin, which] if first else (k_ref, v_ref)[which],
-                dst_ref=out_ref.at[origin, which],
+                src_ref=out[which].at[origin] if first else (k_ref, v_ref)[which],
+                dst_ref=out[which].at[origin],
                 send_sem=send_sem.at[which, 1 + first, step],
                 recv_sem=recv_sem.at[which, 1 + first, step],
                 device_id=(along(1 - which, ctx, step), exp),
@@ -76,7 +77,7 @@
     for which in range(2):
         pass_on(which, 0)
     own = [
-        pltpu.make_async_copy(source, out_ref.at[ctx, which], local_sem.at[which])
+        pltpu.make_async_copy(source, out[which].at[ctx], local_sem.at[which])
         for which, source in enumerate((k_ref, v_ref))
     ]
     for sent in own:
@@ -96,9 +97,9 @@
 def gather_keys(keys, values):
     return pl.pallas_call(
         gather_kernel,
-        out_shape=jax.ShapeDtypeStruct((N_CTX, 2, TOK, 256), jnp.bfloat16),
+        out_shape=[jax.ShapeDtypeStruct((N_CTX, TOK, 256), jnp.bfloat16)] * 2,
         in_specs=[pl.BlockSpec(memory_space=pltpu.VMEM)] * 2,
-        out_specs=pl.BlockSpec(memory_space=pltpu.VMEM),
+        out_specs=[pl.BlockSpec(memory_space=pltpu.VMEM)] * 2,
         scratch_shapes=[
             pltpu.SemaphoreType.DMA((2, 5, 4)),
             pltpu.SemaphoreType.DMA((2, 5, 4)),
@@ -109,95 +110,6 @@
     )(keys, values)
 
 
-def attend_kernel(
-    pos_ref, len_ref, q_ref, kv_ref, gain_ref, att_ref, norm_ref, where_ref, k_win, v_win
-):
-    ctx = lax.axis_index("ctx")
-    for block in range(BLOCKS):
-        where_ref[pos_ref[0, RUN * block] // RUN] = block
-    ends = []
-    total = jnp.int32(0)
-    for doc in range(DOCS):
-        total = total + len_ref[0, doc]
-        ends.append(total)
-
-    def one_run(run, carry):
-        first_block = pos_ref[0, ctx * TOK + run * RUN] // RUN
-        for step in range(WINDOW):
-            block = where_ref[jnp.maximum(first_block - (WINDOW - 1) + step, 0)]
-            rows = pl.ds(pl.multiple_of((block % 2) * RUN, RUN), RUN)
-            k_win[pl.ds(step * RUN, RUN), :] = kv_ref[block // 2, 0, rows, :]
-            v_win[pl.ds(step * RUN, RUN), :] = kv_ref[block // 2, 1, rows, :]
-        own = first_block * RUN + lax.broadcasted_iota(jnp.int32, (RUN, 1), 0)
-        start = jnp.zeros((RUN, 1), jnp.int32)
-        for end in ends:
-            start = jnp.maximum(start, jnp.where(own >= end, end, 0))
-        places = (first_block - (WINDOW - 1)) * RUN + lax.broadcasted_iota(
-            jnp.int32, (RUN, KEYS), 1
-        )
-        visible = (places >= start) & (places <= own)
-        tokens = pl.ds(pl.multiple_of(run * RUN, RUN), RUN)
-
-        def eight_heads(pair, inner):
-            chains = []
-            for part in (2 * pair, 2 * pair + 1):
-                lanes = pl.ds(pl.multiple_of((part // 4) * HD, HD), HD)
-                queries = jnp.concatenate(
-                    [
-                        q_ref[tokens, pl.ds(pl.multiple_of((part * 4 + i) * HD, HD), HD)]
-                        for i in range(4)
-                    ],
-                    axis=0,
-                )
-                scores = lax.dot_general(
-                    queries,
-                    k_win[:, lanes],
-                    (((1,), (1,)), ((), ())),
-                    preferred_element_type=jnp.float32,
-                )
-                chains.append((part, lanes, scores))
-            for part, lanes, scores in chains:
-                scores = jnp.where(visible[None], scores.reshape(4, RUN, KEYS), neg_large)
-                maxima = jnp.max(scores, axis=2, keepdims=True)
-                probs = jnp.exp((scores - maxima) * (1.0 / math.sqrt(HD)))
-                totals = jnp.sum(probs, axis=2, keepdims=True)
-                summed = jnp.dot(
-                    probs.reshape(4 * RUN, KEYS).astype(jnp.bfloat16),
-                    v_win[:, lanes],
-                    preferred_element_type=jnp.float32,
-                )
-                result = (summed.reshape(4, RUN, HD) / totals).astype(jnp.bfloat16)
-                for i in range(4):
-                    att_ref[
-                        tokens, pl.ds(pl.multiple_of((part * 4 + i) * HD, HD), HD)
-                    ] = result[i]
-            return inner
-
-        lax.fori_loop(0, QH // 8, eight_heads, 0)
-        wide = att_ref[tokens, :].astype(jnp.float32)
-        scale = lax.rsqrt(jnp.mean(wide * wide, axis=1, keepdims=True) + norm_eps)
-        norm_ref[tokens, :] = (wide * scale * gain_ref[...]).astype(jnp.bfloat16)
-        return carry
-
-    lax.fori_loop(0, TOK // RUN, one_run, 0)
-
-
-def attend(positions, lengths, queries, gathered, gain):
-    return pl.pallas_call(
-        attend_kernel,
-        out_shape=[jax.ShapeDtypeStruct((TOK, D), jnp.bfloat16)] * 2,
-        in_specs=[pl.BlockSpec(memory_space=pltpu.SMEM)] * 2
-        + [pl.BlockSpec(memory_space=pltpu.VMEM)] * 3,
-        out_specs=[pl.BlockSpec(memory_space=pltpu.VMEM)] * 2,
-        scratch_shapes=[
-            pltpu.SMEM((BLOCKS,), jnp.int32),
-            pltpu.VMEM((KEYS, 256), jnp.bfloat16),
-            pltpu.VMEM((KEYS, 256), jnp.bfloat16),
-        ],
-        name="attend",
-    )(positions, lengths, queries, gathered, gain)
-
-
 CUTS = ((2, (0, 1), 0, 1536), (1, (0, 2), 1536, 1280), (0, (1, 2), 2816, 1280))
 PLANE = 32
 HALF = 16
@@ -255,10 +167,14 @@
 
 
 def moe_kernel(
+    pos_ref,
+    len_ref,
+    q_ref,
+    k_ref,
+    v_ref,
+    gain_ref,
     routes_ref,
     gates_ref,
-    att_ref,
-    norm_ref,
     gate_hbm,
     up_hbm,
     down_hbm,
@@ -269,6 +185,9 @@
     returned_0,
     returned_1,
     returned_2,
+    att_ref,
+    k_win,
+    v_win,
     gate_ref,
     up_ref,
     down_ref,
@@ -333,28 +252,111 @@
 
     lax.fori_loop(1, N_DEV, greet, 0)
 
-    for cut, (axis, plane, first, width) in enumerate(CUTS):
-        shared[cut][0] = norm_ref[:, first : first + width]
-        all_routes[cut, 0] = routes_ref[...]
-        all_gates[cut, 0] = gates_ref[...]
-    pl.semaphore_wait(barrier, 2 * (64 - 27) - 1)
+    blocks_at = [pos_ref[0, RUN * block] // RUN for block in range(BLOCKS)]
+    ends = []
+    total = jnp.int32(0)
+    for doc in range(DOCS):
+        total = total + len_ref[0, doc]
+        ends.append(total)
+
+    def attend_run(run):
+        first_block = pos_ref[0, ctx * TOK + run * RUN] // RUN
+
+        def window(step, carry):
+            wanted = jnp.maximum(first_block - (WINDOW - 1) + step, 0)
+            block = jnp.int32(0)
+            for index, here in enumerate(blocks_at):
+                block = jnp.where(here == wanted, index, block)
+            rows = pl.ds(pl.multiple_of(step * RUN, RUN), RUN)
+            k_win[rows, :] = k_ref[block]
+            v_win[rows, :] = v_ref[block]
+            return carry
+
+        lax.fori_loop(0, WINDOW, window, 0)
+        own = first_block * RUN + lax.broadcasted_iota(jnp.int32, (RUN, 1), 0)
+        start = jnp.zeros((RUN, 1), jnp.int32)
+        for end in ends:
+            start = jnp.maximum(start, jnp.where(own >= end, end, 0))
+        places = (first_block - (WINDOW - 1)) * RUN + lax.broadcasted_iota(
+            jnp.int32, (RUN, KEYS), 1
+        )
+        visible = (places >= start) & (places <= own)
+        tokens = slice(run * RUN, run * RUN + RUN)
+
+        def eight_heads(pair, inner):
+            chains = []
+            for part in (2 * pair, 2 * pair + 1):
+                lanes = pl.ds(pl.multiple_of((part // 4) * HD, HD), HD)
+                queries = jnp.concatenate(
+                    [
+                        q_ref[tokens, pl.ds(pl.multiple_of((part * 4 + i) * HD, HD), HD)]
+                        for i in range(4)
+                    ],
+                    axis=0,
+                )
+                scores = lax.dot_general(
+                    queries,
+                    k_win[:, lanes],
+                    (((1,), (1,)), ((), ())),
+                    preferred_element_type=jnp.float32,
+                )
+                chains.append((part, lanes, scores))
+            for part, lanes, scores in chains:
+                scores = jnp.where(visible[None], scores.reshape(4, RUN, KEYS), neg_large)
+                maxima = jnp.max(scores, axis=2, keepdims=True)
+                probs = jnp.exp((scores - maxima) * (1.0 / math.sqrt(HD)))
+                totals = jnp.sum(probs, axis=2, keepdims=True)
+                summed = jnp.dot(
+                    probs.reshape(4 * RUN, KEYS).astype(jnp.bfloat16),
+                    v_win[:, lanes],
+                    preferred_element_type=jnp.float32,
+                )
+                result = (summed.reshape(4, RUN, HD) / totals).astype(jnp.bfloat16)
+                for i in range(4):
+                    att_ref[
+                        tokens, pl.ds(pl.multiple_of((part * 4 + i) * HD, HD), HD)
+                    ] = result[i]
+            return inner
+
+        lax.fori_loop(0, QH // 8, eight_heads, 0)
+        wide = att_ref[tokens, :].astype(jnp.float32)
+        scale = lax.rsqrt(jnp.mean(wide * wide, axis=1, keepdims=True) + norm_eps)
+        for cut, (axis, plane, first, width) in enumerate(CUTS):
+            span = slice(first, first + width)
+            shared[cut][0, tokens, :] = (wide[:, span] * scale * gain_ref[:, span]).astype(
+                jnp.bfloat16
+            )
 
     def line_copy(cut, kind, step):
-        ref = (all_routes.at[cut], all_gates.at[cut], shared[cut])[kind]
+        if kind < 2:
+            ref = (all_routes, all_gates)[kind].at[cut]
+            source, target = ref.at[0], ref.at[step]
+        else:
+            run = pl.ds((kind - 2) * RUN, RUN)
+            source, target = shared[cut].at[0, run], shared[cut].at[step, run]
         return pltpu.make_async_remote_copy(
-            src_ref=ref.at[0],
-            dst_ref=ref.at[step],
+            src_ref=source,
+            dst_ref=target,
             send_sem=line_send.at[cut, kind, step],
             recv_sem=line_recv.at[cut, kind, step],
             device_id=shift(ctx, exp, line_steps(CUTS[cut][0], step)),
             device_id_type=MESH,
         )
 
-    line_copies = [
-        (cut, kind, step) for kind in range(3) for step in (1, 3, 2) for cut in range(3)
-    ]
-    for which in line_copies:
-        line_copy(*which).start()
+    def share(kinds):
+        for kind in kinds:
+            for step in (1, 3, 2):
+                for cut in range(3):
+                    line_copy(cut, kind, step).start()
+
+    for cut in range(3):
+        all_routes[cut, 0] = routes_ref[...]
+        all_gates[cut, 0] = gates_ref[...]
+    attend_run(0)
+    pl.semaphore_wait(barrier, 2 * (64 - 27) - 1)
+    share((0, 1, 2))
+    attend_run(1)
+    share((3,))
     for load in loads:
         load.start()
 
@@ -468,10 +470,15 @@
         own_out(cut).start()
 
     early = 4
+    for step in (1, 3):
+        for cut in every:
+            line_copy(cut, 2, step).wait()
+            line_copy(cut, 3, step).wait()
+            pack_main(cut, step)
     for cut in every:
-        for step in (1, 3, 2):
-            line_copy(cut, 2, step).wait()
-        sources(cut, 1, 4, pack_main)
+        line_copy(cut, 2, 2).wait()
+        line_copy(cut, 3, 2).wait()
+        pack_main(cut, 2)
         pack_extra(cut)
         each(0, (cut,), send, send_own, 0, early)
     each(0, every, send, send_own, early, HALF)
@@ -565,6 +572,20 @@
 
             def answer(k, inner):
                 slot = base + pair * 8 + (k * 3) % 8
+                later = base + ((2 * k) * 7) % HALF
+                last = base + ((2 * k + 1) * 7) % HALF
+
+                @pl.when(pair == 1)
+                def _():
+                    @pl.when(later > 0)
+                    def _():
+                        homeward(2, later).start()
+
+                    @pl.when(later == 0)
+                    def _():
+                        own_back(2).start()
+
+                    homeward(2, last).start()
 
                 @pl.when(slot > 0)
                 def _():
@@ -582,7 +603,6 @@
             return inner
 
         lax.fori_loop(0, 2, two_z, 0)
-        each(half, (2,), lambda cut, slot: homeward(cut, slot).start(), lambda cut: own_back(cut).start())
         return carry
 
     lax.fori_loop(0, 2, expert_half, 0)
@@ -592,18 +612,15 @@
         return pltpu.make_async_remote_copy(
             src_ref=shared[cut].at[source],
             dst_ref=collect[cut].at[source - 1],
-            send_sem=line_send.at[cut, 3, source],
-            recv_sem=line_recv.at[cut, 3, source],
+            send_sem=line_send.at[cut, 4, source],
+            recv_sem=line_recv.at[cut, 4, source],
             device_id=shift(ctx, exp, line_steps(axis, 4 - source)),
             device_id_type=MESH,
         )
 
     def answers(cut, half):
         first, width = CUTS[cut][2:]
-        each(half, (cut,), lambda c, slot: homeward(c, slot).wait(), lambda c: own_back(c).wait())
-        copy = fetch(returned, cut, half)
-        copy.start()
-        copy.wait()
+        fetch(returned, cut, half).wait()
 
         def one(source, carry):
             span = pl.ds(half * HALF, HALF)
@@ -640,13 +657,23 @@
 
         lax.fori_loop(0, 4, one, 0)
 
+    def arrive(cut, half):
+        each(half, (cut,), lambda c, slot: homeward(c, slot).wait(), lambda c: own_back(c).wait())
+        fetch(returned, cut, half).start()
+
+    for cut in every:
+        arrive(cut, 0)
     for cut in every:
         answers(cut, 0)
+    arrive(0, 1)
+    arrive(1, 1)
     for cut, (axis, plane, first, width) in enumerate(CUTS):
         answers(cut, 1)
         for source in (1, 3, 2):
             shared[cut][source] = part_sum[source, :, first : first + width].astype(jnp.bfloat16)
             collect_copy(cut, source).start()
+        if cut == 0:
+            arrive(2, 1)
     for cut, (axis, plane, first, width) in enumerate(CUTS):
         span = slice(first, first + width)
         total = att_ref[:, span].astype(jnp.float32) + part_sum[0, :, span]
@@ -656,7 +683,7 @@
         out_ref[:, span] = total.astype(jnp.bfloat16)
 
 
-def moe(routes, gates, attended, normed, gate, up, down):
+def moe(positions, lengths, queries, keys, values, gain, routes, gates, gate, up, down):
     vmem = pl.BlockSpec(memory_space=pltpu.VMEM)
     hbm = pl.BlockSpec(memory_space=pltpu.HBM)
     widths = [width for axis, plane, first, width in CUTS]
@@ -665,9 +692,12 @@
         moe_kernel,
         out_shape=[jax.ShapeDtypeStruct((TOK, D), jnp.bfloat16)]
         + [jax.ShapeDtypeStruct(shape, jnp.bfloat16) for shape in wire] * 2,
-        in_specs=[vmem] * 4 + [hbm] * 3,
+        in_specs=[pl.BlockSpec(memory_space=pltpu.SMEM)] * 2 + [vmem] * 6 + [hbm] * 3,
         out_specs=[vmem] + [hbm] * 6,
         scratch_shapes=[
+            pltpu.VMEM((TOK, D), jnp.bfloat16),
+            pltpu.VMEM((KEYS, 256), jnp.bfloat16),
+            pltpu.VMEM((KEYS, 256), jnp.bfloat16),
             pltpu.VMEM((D, HID), jnp.bfloat16),
             pltpu.VMEM((D, HID), jnp.bfloat16),
             pltpu.VMEM((HID, D), jnp.bfloat16),
@@ -682,8 +712,8 @@
             pltpu.VMEM((3, 4, PLANE, TOK), jnp.int32),
             pltpu.VMEM((3, 4, PLANE, TOK), jnp.float32),
             pltpu.VMEM((4, TOK, D), jnp.float32),
-            pltpu.SemaphoreType.DMA((3, 4, 4)),
-            pltpu.SemaphoreType.DMA((3, 4, 4)),
+            pltpu.SemaphoreType.DMA((3, 5, 4)),
+            pltpu.SemaphoreType.DMA((3, 5, 4)),
             pltpu.SemaphoreType.DMA((3, PLANE)),
             pltpu.SemaphoreType.DMA((3, PLANE)),
             pltpu.SemaphoreType.DMA((3, PLANE)),
@@ -694,7 +724,7 @@
             collective_id=1, has_side_effects=True, vmem_limit_bytes=62 << 20
         ),
         name="moe",
-    )(routes, gates, attended, normed, gate, up, down)[0]
+    )(positions, lengths, queries, keys, values, gain, routes, gates, gate, up, down)[0]
 
 
 def local(
@@ -710,15 +740,16 @@
     up_proj,
     down_proj,
 ):
-    gathered = gather_keys(key_states[0], value_states[0])
-    attended, normed = attend(
-        positions, lengths, query_states[0], gathered, norm_gain.reshape(1, D)
-    )
+    keys, values = gather_keys(key_states[0], value_states[0])
     out = moe(
+        positions,
+        lengths,
+        query_states[0],
+        keys.reshape(BLOCKS, RUN, 256),
+        values.reshape(BLOCKS, RUN, 256),
+        norm_gain.reshape(1, D),
         routes[0].T,
         gate_weights[0].T,
-        attended,
-        normed,
         gate_proj[0],
         up_proj[0],
         down_proj[0],

time: 274 us -> 254 us (0.927); the launches traced: 269 us -> 253 us
  Pallas kernels: 267 us -> 251 us
    pallas_call x2 -> x1, Pallas kernels: 34.2 us -> 23.5 us  [gather_keys(): pl.pallas_call(gather_kernel, out_shape=[jax.ShapeDtypeStruct((N_CTX, TOK...]
    pallas_call x1, Pallas kernels: 233 us -> 227 us  [moe(): pl.pallas_call(moe_kernel, out_shape=[jax.ShapeDtypeStruct((TOK, D), jnp....]
where the time goes in v5:
time: 254 us; the launch traced here: 253 us
  Pallas kernels  251 us (99%)
    pallas_call x1, Pallas kernels, moe(): pl.pallas_call(moe_kernel, out_shape=[jax.ShapeDtypeStruct((TOK, D), jnp....  227 us
    pallas_call x1, Pallas kernels, gather_keys(): pl.pallas_call(gather_kernel, out_shape=[jax.ShapeDtypeStruct((N_CTX, TOK...  23.5 us

profile of v5, /device:TPU:32, one launch (start us, length us, event | category | flops | bytes accessed | tf_op | source)
XLA Modules:
  0.0 253.2 jit_solution(1720837693902941176)
XLA Ops:
  0.0 23.5 %gather_keys.1 = (bf16[16,128,256]{2,1,0:T(8,128)(2,1)}, bf16[16,128,256]{2,1,0:T(8,128)(2,1)}) custom-call(bf16[128,256]{1,0:T(8,128)(2,1)} %bitcast.23, bf16[128,256]{1,0:T(8,128)(2,1)} %bitcast.24), custom_call_target="tpu_custom_call" | custom-call | tf_op jit(solution)/shard_map/gather_keys/pallas_call | solution.py:98
  23.6 227.3 %moe.1 = (bf16[128,4096]{1,0:T(8,128)(2,1)}, bf16[32,5,8,1536]{3,2,1,0:T(8,128)(2,1)}, bf16[32,5,8,1280]{3,2,1,0:T(8,128)(2,1)}, bf16[32,5,8,1280]{3,2,1,0:T(8,1...) custom-call(s32[1,2048]{1,0:T(1,128)} %pos_ref.1, ...), custom_call_target="tpu_custom_call" | custom-call | tf_op jit(solution)/shard_map/moe/pallas_call | solution.py:691
  250.9 2.3 copy.13

commit v6 on v5

--- a/solution.py
+++ b/solution.py
@@ -492,8 +492,13 @@
         )
 
     def expert_half(half, carry):
-        each(half, every, lambda cut, slot: outward(cut, slot).wait(), lambda cut: own_out(cut).wait())
         for cut in every:
+            each(
+                half,
+                (cut,),
+                lambda which, slot: outward(which, slot).wait(),
+                lambda which: own_out(which).wait(),
+            )
             fetch(arrived, cut, half).start()
         for cut in every:
             fetch(arrived, cut, half).wait()
@@ -618,62 +623,70 @@
             device_id_type=MESH,
         )
 
-    def answers(cut, half):
-        first, width = CUTS[cut][2:]
-        fetch(returned, cut, half).wait()
-
-        def one(source, carry):
-            span = pl.ds(half * HALF, HALF)
-            slots = slot_ref[cut, source, span, :]
-            weights = jnp.broadcast_to(
-                weight_ref[cut, source, span, :][:, None, :], (HALF, 8, TOK)
-            ).reshape(HALF * 8, TOK)
-            value = jnp.concatenate(
-                [
-                    jnp.where(main_hits(slots, HALF), weights, 0.0),
-                    jnp.where(extra_hits(slots, HALF, source), weights, 0.0),
-                ],
-                axis=0,
-            )
-            high = value.astype(jnp.bfloat16)
-            low = (value - high.astype(jnp.float32)).astype(jnp.bfloat16)
-            factors = jnp.concatenate([high, low], axis=1)
-            rows = jnp.concatenate(
-                [
-                    stage[cut][:, source].reshape(HALF * 8, width),
-                    stage[cut][:, 4].reshape(HALF * 8, width),
-                ],
-                axis=0,
-            )
-            both = lax.dot_general(
-                factors, rows, (((0,), (0,)), ((), ())), preferred_element_type=jnp.float32
-            )
-            total = both[:TOK] + both[TOK:]
-            if half == 0:
-                part_sum[source, :, first : first + width] = total
-            else:
-                part_sum[source, :, first : first + width] += total
-            return carry
-
-        lax.fori_loop(0, 4, one, 0)
+    def answers(cut, half, source):
+        width = CUTS[cut][3]
+        span = pl.ds(half * HALF, HALF)
+        slots = slot_ref[cut, source, span, :]
+        weights = jnp.broadcast_to(
+            weight_ref[cut, source, span, :][:, None, :], (HALF, 8, TOK)
+        ).reshape(HALF * 8, TOK)
+        value = jnp.concatenate(
+            [
+                jnp.where(main_hits(slots, HALF), weights, 0.0),
+                jnp.where(extra_hits(slots, HALF, source), weights, 0.0),
+            ],
+            axis=0,
+        )
+        high = value.astype(jnp.bfloat16)
+        low = (value - high.astype(jnp.float32)).astype(jnp.bfloat16)
+        factors = jnp.concatenate([high, low], axis=1)
+        rows = jnp.concatenate(
+            [
+                stage[cut][:, source].reshape(HALF * 8, width),
+                stage[cut][:, 4].reshape(HALF * 8, width),
+            ],
+            axis=0,
+        )
+        both = lax.dot_general(
+            factors, rows, (((0,), (0,)), ((), ())), preferred_element_type=jnp.float32
+        )
+        return both[:TOK] + both[TOK:]
+
+    def columns(cut):
+        return slice(CUTS[cut][2], CUTS[cut][2] + CUTS[cut][3])
+
+    def first_sums(cut, source):
+        part_sum[source, :, columns(cut)] = answers(cut, 0, source)
 
     def arrive(cut, half):
         each(half, (cut,), lambda c, slot: homeward(c, slot).wait(), lambda c: own_back(c).wait())
         fetch(returned, cut, half).start()
 
+    def send_sums(cut):
+        fetch(returned, cut, 1).wait()
+
+        def one(k, carry):
+            source = 1 + (k + 1) % 3
+            total = part_sum[source, :, columns(cut)] + answers(cut, 1, source)
+            shared[cut][source] = total.astype(jnp.bfloat16)
+            collect_copy(cut, source).start()
+            return carry
+
+        lax.fori_loop(0, 3, one, 0)
+
     for cut in every:
         arrive(cut, 0)
     for cut in every:
-        answers(cut, 0)
+        fetch(returned, cut, 0).wait()
+        sources(cut, 0, 4, first_sums)
     arrive(0, 1)
     arrive(1, 1)
-    for cut, (axis, plane, first, width) in enumerate(CUTS):
-        answers(cut, 1)
-        for source in (1, 3, 2):
-            shared[cut][source] = part_sum[source, :, first : first + width].astype(jnp.bfloat16)
-            collect_copy(cut, source).start()
-        if cut == 0:
-            arrive(2, 1)
+    send_sums(0)
+    arrive(2, 1)
+    send_sums(1)
+    send_sums(2)
+    for cut in every:
+        part_sum[0, :, columns(cut)] += answers(cut, 1, 0)
     for cut, (axis, plane, first, width) in enumerate(CUTS):
         span = slice(first, first + width)
         total = att_ref[:, span].astype(jnp.float32) + part_sum[0, :, span]

time: 254 us -> 252 us (level)
  no operation moved by 1% of the time
where the time goes in v6:
time: 252 us; the launch traced here: 251 us
  Pallas kernels  249 us (99%)
    pallas_call x1, Pallas kernels, moe(): pl.pallas_call(moe_kernel, out_shape=[jax.ShapeDtypeStruct((TOK, D), jnp....  225 us
    pallas_call x1, Pallas kernels, gather_keys(): pl.pallas_call(gather_kernel, out_shape=[jax.ShapeDtypeStruct((N_CTX, TOK...  23.5 us

profile of v6, /device:TPU:32, one launch (start us, length us, event | category | flops | bytes accessed | tf_op | source)
XLA Modules:
  0.0 251.3 jit_solution(8140562050804833778)
XLA Ops:
  0.0 23.5 %gather_keys.1 = (bf16[16,128,256]{2,1,0:T(8,128)(2,1)}, bf16[16,128,256]{2,1,0:T(8,128)(2,1)}) custom-call(bf16[128,256]{1,0:T(8,128)(2,1)} %bitcast.23, bf16[128,256]{1,0:T(8,128)(2,1)} %bitcast.24), custom_call_target="tpu_custom_call" | custom-call | tf_op jit(solution)/shard_map/gather_keys/pallas_call | solution.py:98
  23.6 225.4 %moe.1 = (bf16[128,4096]{1,0:T(8,128)(2,1)}, bf16[32,5,8,1536]{3,2,1,0:T(8,128)(2,1)}, bf16[32,5,8,1280]{3,2,1,0:T(8,128)(2,1)}, bf16[32,5,8,1280]{3,2,1,0:T(8,1...) custom-call(s32[1,2048]{1,0:T(1,128)} %pos_ref.1, ...), custom_call_target="tpu_custom_call" | custom-call | tf_op jit(solution)/shard_map/moe/pallas_call | solution.py:704
  249.0 2.3 copy.13

commit v7 on v6

--- a/solution.py
+++ b/solution.py
@@ -578,7 +578,6 @@
             def answer(k, inner):
                 slot = base + pair * 8 + (k * 3) % 8
                 later = base + ((2 * k) * 7) % HALF
-                last = base + ((2 * k + 1) * 7) % HALF
 
                 @pl.when(pair == 1)
                 def _():
@@ -590,8 +589,6 @@
                     def _():
                         own_back(2).start()
 
-                    homeward(2, last).start()
-
                 @pl.when(slot > 0)
                 def _():
                     homeward(0, slot).start()
@@ -604,7 +601,16 @@
 
                 return inner
 
+            def answer_last(k, inner):
+                homeward(2, base + ((2 * k + 1) * 7) % HALF).start()
+                return inner
+
             lax.fori_loop(0, 8, answer, 0)
+
+            @pl.when(pair == 1)
+            def _():
+                lax.fori_loop(0, 8, answer_last, 0)
+
             return inner
 
         lax.fori_loop(0, 2, two_z, 0)

time: 252 us -> 257 us (1.020)
  Pallas kernels: 249 us -> 253 us
    pallas_call x1, Pallas kernels: 225 us -> 230 us  [moe(): pl.pallas_call(moe_kernel, out_shape=[jax.ShapeDtypeStruct((TOK, D), jnp....]
where the time goes in v7:
time: 257 us; the launch traced here: 255 us
  Pallas kernels  253 us (98%)
    pallas_call x1, Pallas kernels, moe(): pl.pallas_call(moe_kernel, out_shape=[jax.ShapeDtypeStruct((TOK, D), jnp....  230 us
    pallas_call x1, Pallas kernels, gather_keys(): pl.pallas_call(gather_kernel, out_shape=[jax.ShapeDtypeStruct((N_CTX, TOK...  23.5 us

profile of v7, /device:TPU:32, one launch (start us, length us, event | category | flops | bytes accessed | tf_op | source)
XLA Modules:
  0.0 255.5 jit_solution(702883771048685776)
XLA Ops:
  0.0 23.5 %gather_keys.1 = (bf16[16,128,256]{2,1,0:T(8,128)(2,1)}, bf16[16,128,256]{2,1,0:T(8,128)(2,1)}) custom-call(bf16[128,256]{1,0:T(8,128)(2,1)} %bitcast.23, bf16[128,256]{1,0:T(8,128)(2,1)} %bitcast.24), custom_call_target="tpu_custom_call" | custom-call | tf_op jit(solution)/shard_map/gather_keys/pallas_call | solution.py:98
  23.6 229.6 %moe.1 = (bf16[128,4096]{1,0:T(8,128)(2,1)}, bf16[32,5,8,1536]{3,2,1,0:T(8,128)(2,1)}, bf16[32,5,8,1280]{3,2,1,0:T(8,128)(2,1)}, bf16[32,5,8,1280]{3,2,1,0:T(8,1...) custom-call(s32[1,2048]{1,0:T(1,128)} %pos_ref.1, ...), custom_call_target="tpu_custom_call" | custom-call | tf_op jit(solution)/shard_map/moe/pallas_call | solution.py:710
  253.2 2.3 copy.13
